TPU v7x, 32 devices: a whole 2x2x4 slice. The times are simulated.
32 devices in a mesh: row: 4 (over z), col: 8 (over y, x, core).
Axes of the slice: x: 2, y: 2, z: 4, core: 2. Of those that a mesh axis runs over, the one named last changes fastest.
Arguments:
- rhs: bfloat16 [4, 8, 128, 1024], P('row', 'col'), may hold values from -6 to 6
- operators: bfloat16 [4, 8, 3, 1024, 1024], P('row', 'col'), may hold values from -0.09375 to 0.09375
- positions: int32 [128], replicated, may hold values from 0 to 32767
- start_tick: int32 [128], replicated, may hold values from 0 to 7
Outputs:
- traces: bfloat16 [4, 8, 128, 1024], P('row', 'col')
All inputs are finite; a program needn't handle non-finite values.
Results may differ from a plain program's by a relative error of at most 0.006.
Values may be sent and summed in bfloat16 or wider, within the bound.
No kernel may reach another device: no remote copies, remote signals or barrier semaphores. Data moves between devices by JAX's collectives and lax.ppermute only.
A program may use at most 64 MiB of HBM per device.

v0:
```python
import jax
import jax.numpy as jnp
from jax import lax
from jax.sharding import PartitionSpec as P

TICKS = 8


def passed_along(block, axis, distance):
    devices = range(lax.axis_size(axis))
    route = [(i - distance, i) for i in devices if i - distance in devices]
    return lax.ppermute(block, axis, route)


def incoming(traces, sign):
    col_count = lax.axis_size("col")
    from_row = passed_along(traces, "row", sign)
    from_col = passed_along(traces, "col", sign)
    arrived = passed_along(traces, ("row", "col"), sign * (col_count + 1))
    source_col = lax.axis_index("col") - sign
    inside = jnp.logical_and(source_col >= 0, source_col < col_count)
    diagonal_in = jnp.where(inside, arrived, jnp.zeros_like(arrived))
    return (from_row, from_col, diagonal_in)


def body(rhs, operators, positions, start_tick):
    batches = rhs.shape[2]
    trace_width = rhs.shape[3]
    operator_set = operators[0, 0]
    device_flat = lax.axis_index("row") * lax.axis_size("col") + lax.axis_index("col")
    local_point = positions - device_flat * trace_width
    column_ids = lax.broadcasted_iota(jnp.int32, (batches, trace_width), 1)
    spike_mask = (local_point[:, None] == column_ids).astype(jnp.float32)
    source = rhs[0, 0].astype(jnp.float32) + 4.0 * spike_mask
    traces = jnp.zeros((batches, trace_width), jnp.bfloat16)
    turning = TICKS // 2
    for tick_index in range(TICKS):
        summed = source
        if tick_index > 0:
            sign = 1 if tick_index < turning else -1
            from_row, from_col, diagonal_in = incoming(traces, sign)
            summed = summed + jnp.dot(from_row, operator_set[0], preferred_element_type=jnp.float32)
            summed = summed + jnp.dot(from_col, operator_set[1], preferred_element_type=jnp.float32)
            summed = summed + jnp.dot(
                diagonal_in, operator_set[2], preferred_element_type=jnp.float32
            )
        running = (tick_index >= start_tick)[:, None]
        traces = jnp.where(running, summed, 0.0).astype(jnp.bfloat16)
    return traces[None, None]


def solution(mesh):
    placed = (P("row", "col", None, None), P("row", "col", None, None, None), P(), P())
    return jax.shard_map(
        body, mesh=mesh, in_specs=placed, out_specs=P("row", "col", None, None), check_vma=False
    )
```

profile of v0, /device:TPU:1, one launch (start us, length us, event | category | flops | bytes accessed | tf_op | source)
XLA Modules:
  0.0 135.1 jit_solution(11262018170523809969)
XLA Ops:
  2.6 4.5 %collective-permute-start.1 = (bf16[128,1024]{1,0:T(8,128)(2,1)S(1)}, bf16[128,1024]{1,0:T(8,128)(2,1)S(1)}, u32[]{:S(2)}, u32[]{:S(2)}) collective-permute-start(bf16[128,1024]{1,0:T(8,128)(2,1)S(1)} %select_convert_fusion), channel_id=1, source_target_pairs={{0,1},{1,2},{2,3},{3,4},{4,5},{5,6},{6,7},{8,9},{9,10},{10,11},{11... | collective-permute-start | bytes 786440 | tf_op jit(solution)/shard_map/ppermute | solution.py:12
  7.1 2.9 %collective-permute-start.2 = (bf16[128,1024]{1,0:T(8,128)(2,1)S(1)}, bf16[128,1024]{1,0:T(8,128)(2,1)S(1)}, u32[]{:S(2)}, u32[]{:S(2)}) collective-permute-start(bf16[128,1024]{1,0:T(8,128)(2,1)S(1)} %select_convert_fusion), channel_id=1, source_target_pairs={{0,9},{1,10},{2,11},{3,12},{4,13},{5,14},{6,15},{7,16},{8,17},{9,1... | collective-permute-start | bytes 786440 | tf_op jit(solution)/shard_map/ppermute | solution.py:12
  10.0 3.2 %collective-permute-start = (bf16[128,1024]{1,0:T(8,128)(2,1)S(1)}, bf16[128,1024]{1,0:T(8,128)(2,1)S(1)}, u32[]{:S(2)}, u32[]{:S(2)}) collective-permute-start(bf16[128,1024]{1,0:T(8,128)(2,1)S(1)} %select_convert_fusion), channel_id=1, source_target_pairs={{0,8},{8,16},{16,24},{1,9},{9,17},{17,25},{2,10},{10,18},{18,26},{... | collective-permute-start | bytes 786440 | tf_op jit(solution)/shard_map/ppermute | solution.py:12
  13.3 2.2 %fusion.26 = f32[128,1024]{1,0:T(8,128)S(1)} fusion(bf16[128,1024]{1,0:T(8,128)(2,1)S(1)} %collective-permute-done.1, bf16[1,1,3,1024,1024]{4,3,2,1,0:T(8,128)(2,1)} %param.5), kind=kOutput, calls=%fused_computation.26 | convolution fusion | flops 268435456 | bytes 2883584 | tf_op jit(solution)/shard_map/dot_general | solution.py:43
  15.5 2.3 %fusion.12 = f32[128,1024]{1,0:T(8,128)S(1)} fusion(bf16[1,1,3,1024,1024]{4,3,2,1,0:T(8,128)(2,1)} %param.5, bf16[128,1024]{1,0:T(8,128)(2,1)S(1)} %collective-permute-done.2, pred[]{:T(512)S(6)} %and.6), kind=kOutput, calls=%fused_computation.12 | convolution fusion | flops 268566528 | bytes 2883585 | tf_op jit(solution)/shard_map/dot_general | solution.py:44
  17.7 3.2 %collective-permute-done = bf16[128,1024]{1,0:T(8,128)(2,1)S(1)} collective-permute-done((bf16[128,1024]{1,0:T(8,128)(2,1)S(1)}, bf16[128,1024]{1,0:T(8,128)(2,1)S(1)}, u32[]{:S(2)}, u32[]{:S(2)}) %collective-permute-start) | collective-permute-done | bytes 262176 | tf_op jit(solution)/shard_map/ppermute | solution.py:12
  21.4 6.2 %collective-permute-start.5 = (bf16[128,1024]{1,0:T(8,128)(2,1)S(1)}, bf16[128,1024]{1,0:T(8,128)(2,1)S(1)}, u32[]{:S(2)}, u32[]{:S(2)}) collective-permute-start(bf16[128,1024]{1,0:T(8,128)(2,1)S(1)} %fusion.144), channel_id=1, source_target_pairs={{0,9},{1,10},{2,11},{3,12},{4,13},{5,14},{6,15},{7,16},{8,17},{9,1... | collective-permute-start | bytes 786440 | tf_op jit(solution)/shard_map/ppermute | solution.py:12
  27.6 1.9 %collective-permute-start.4 = (bf16[128,1024]{1,0:T(8,128)(2,1)S(1)}, bf16[128,1024]{1,0:T(8,128)(2,1)S(1)}, u32[]{:S(2)}, u32[]{:S(2)}) collective-permute-start(bf16[128,1024]{1,0:T(8,128)(2,1)S(1)} %fusion.144), channel_id=1, source_target_pairs={{0,1},{1,2},{2,3},{3,4},{4,5},{5,6},{6,7},{8,9},{9,10},{10,11},{11... | collective-permute-start | bytes 786440 | tf_op jit(solution)/shard_map/ppermute | solution.py:12
  29.5 3.2 %collective-permute-start.3 = (bf16[128,1024]{1,0:T(8,128)(2,1)S(1)}, bf16[128,1024]{1,0:T(8,128)(2,1)S(1)}, u32[]{:S(2)}, u32[]{:S(2)}) collective-permute-start(bf16[128,1024]{1,0:T(8,128)(2,1)S(1)} %fusion.144), channel_id=1, source_target_pairs={{0,8},{8,16},{16,24},{1,9},{9,17},{17,25},{2,10},{10,18},{18,26},{... | collective-permute-start | bytes 786440 | tf_op jit(solution)/shard_map/ppermute | solution.py:12
  33.7 4.2 %collective-permute-done.3 = bf16[128,1024]{1,0:T(8,128)(2,1)S(1)} collective-permute-done((bf16[128,1024]{1,0:T(8,128)(2,1)S(1)}, bf16[128,1024]{1,0:T(8,128)(2,1)S(1)}, u32[]{:S(2)}, u32[]{:S(2)}) %collective-permute-start.3) | collective-permute-done | bytes 262176 | tf_op jit(solution)/shard_map/ppermute | solution.py:12
  38.4 6.3 %collective-permute-start.8 = (bf16[128,1024]{1,0:T(8,128)(2,1)S(1)}, bf16[128,1024]{1,0:T(8,128)(2,1)S(1)}, u32[]{:S(2)}, u32[]{:S(2)}) collective-permute-start(bf16[128,1024]{1,0:T(8,128)(2,1)S(1)} %fusion.141), channel_id=1, source_target_pairs={{0,9},{1,10},{2,11},{3,12},{4,13},{5,14},{6,15},{7,16},{8,17},{9,1... | collective-permute-start | bytes 786440 | tf_op jit(solution)/shard_map/ppermute | solution.py:12
  44.7 1.9 %collective-permute-start.7 = (bf16[128,1024]{1,0:T(8,128)(2,1)S(1)}, bf16[128,1024]{1,0:T(8,128)(2,1)S(1)}, u32[]{:S(2)}, u32[]{:S(2)}) collective-permute-start(bf16[128,1024]{1,0:T(8,128)(2,1)S(1)} %fusion.141), channel_id=1, source_target_pairs={{0,1},{1,2},{2,3},{3,4},{4,5},{5,6},{6,7},{8,9},{9,10},{10,11},{11... | collective-permute-start | bytes 786440 | tf_op jit(solution)/shard_map/ppermute | solution.py:12
  46.6 3.2 %collective-permute-start.6 = (bf16[128,1024]{1,0:T(8,128)(2,1)S(1)}, bf16[128,1024]{1,0:T(8,128)(2,1)S(1)}, u32[]{:S(2)}, u32[]{:S(2)}) collective-permute-start(bf16[128,1024]{1,0:T(8,128)(2,1)S(1)} %fusion.141), channel_id=1, source_target_pairs={{0,8},{8,16},{16,24},{1,9},{9,17},{17,25},{2,10},{10,18},{18,26},{... | collective-permute-start | bytes 786440 | tf_op jit(solution)/shard_map/ppermute | solution.py:12
  50.8 4.2 %collective-permute-done.6 = bf16[128,1024]{1,0:T(8,128)(2,1)S(1)} collective-permute-done((bf16[128,1024]{1,0:T(8,128)(2,1)S(1)}, bf16[128,1024]{1,0:T(8,128)(2,1)S(1)}, u32[]{:S(2)}, u32[]{:S(2)}) %collective-permute-start.6) | collective-permute-done | bytes 262176 | tf_op jit(solution)/shard_map/ppermute | solution.py:12
  55.5 3.4 %collective-permute-start.10 = (bf16[128,1024]{1,0:T(8,128)(2,1)S(1)}, bf16[128,1024]{1,0:T(8,128)(2,1)S(1)}, u32[]{:S(2)}, u32[]{:S(2)}) collective-permute-start(bf16[128,1024]{1,0:T(8,128)(2,1)S(1)} %fusion.138), channel_id=1, source_target_pairs={{1,0},{2,1},{3,2},{4,3},{5,4},{6,5},{7,6},{9,8},{10,9},{11,10},{12... | collective-permute-start | bytes 786440 | tf_op jit(solution)/shard_map/ppermute | solution.py:12
  61.5 2.1 %collective-permute-done.10 = bf16[128,1024]{1,0:T(8,128)(2,1)S(1)} collective-permute-done((bf16[128,1024]{1,0:T(8,128)(2,1)S(1)}, bf16[128,1024]{1,0:T(8,128)(2,1)S(1)}, u32[]{:S(2)}, u32[]{:S(2)}) %collective-permute-start.10) | collective-permute-done | bytes 262176 | tf_op jit(solution)/shard_map/ppermute | solution.py:12
  63.6 2.0 %fusion.20 = f32[128,1024]{1,0:T(8,128)S(1)} fusion(bf16[128,1024]{1,0:T(8,128)(2,1)S(1)} %collective-permute-done.10, bf16[1,1,3,1024,1024]{4,3,2,1,0:T(8,128)(2,1)} %param.5), kind=kOutput, calls=%fused_computation.20 | convolution fusion | flops 268435456 | bytes 2883584 | tf_op jit(solution)/shard_map/dot_general | solution.py:43
  65.7 4.7 %collective-permute-done.11 = bf16[128,1024]{1,0:T(8,128)(2,1)S(1)} collective-permute-done((bf16[128,1024]{1,0:T(8,128)(2,1)S(1)}, bf16[128,1024]{1,0:T(8,128)(2,1)S(1)}, u32[]{:S(2)}, u32[]{:S(2)}) %collective-permute-start.11) | collective-permute-done | bytes 262176 | tf_op jit(solution)/shard_map/ppermute | solution.py:12
  70.3 2.0 %fusion.6 = f32[128,1024]{1,0:T(8,128)S(1)} fusion(bf16[1,1,3,1024,1024]{4,3,2,1,0:T(8,128)(2,1)} %param.5, bf16[128,1024]{1,0:T(8,128)(2,1)S(1)} %collective-permute-done.11, pred[]{:T(512)S(6)} %and.14), kind=kOutput, calls=%fused_computation.6 | convolution fusion | flops 268566528 | bytes 2883585 | tf_op jit(solution)/shard_map/dot_general | solution.py:44
  72.4 2.5 %collective-permute-done.9 = bf16[128,1024]{1,0:T(8,128)(2,1)S(1)} collective-permute-done((bf16[128,1024]{1,0:T(8,128)(2,1)S(1)}, bf16[128,1024]{1,0:T(8,128)(2,1)S(1)}, u32[]{:S(2)}, u32[]{:S(2)}) %collective-permute-start.9) | collective-permute-done | bytes 262176 | tf_op jit(solution)/shard_map/ppermute | solution.py:12
  74.9 2.1 %fusion.135 = bf16[128,1024]{1,0:T(8,128)(2,1)S(1)} fusion(f32[128,1024]{1,0:T(8,128)S(1)} %fusion.6, f32[128,1024]{1,0:T(8,128)S(1)} %fusion.20, bf16[128,1024]{1,0:T(8,128)(2,1)S(1)} %collective-permute-done.9, bf16[1,1,3,1024,1024]{4,3,2,1,0:T(8,128)(2,1)} %param.5, bf16[1,1,128,1024]{3,2,1,0:T(8,128)(2,1)S(1)} %copy-done, ...), kind=kOutput, calls=%fused_computation.73 | convolution fusion | flops 269615104 | bytes 3932800 | tf_op jit(solution)/shard_map/dot_general | solution.py:42
  78.3 1.9 %collective-permute-start.13 = (bf16[128,1024]{1,0:T(8,128)(2,1)S(1)}, bf16[128,1024]{1,0:T(8,128)(2,1)S(1)}, u32[]{:S(2)}, u32[]{:S(2)}) collective-permute-start(bf16[128,1024]{1,0:T(8,128)(2,1)S(1)} %fusion.135), channel_id=1, source_target_pairs={{1,0},{2,1},{3,2},{4,3},{5,4},{6,5},{7,6},{9,8},{10,9},{11,10},{12... | collective-permute-start | bytes 786440 | tf_op jit(solution)/shard_map/ppermute | solution.py:12
  81.6 6.9 %collective-permute-done.14 = bf16[128,1024]{1,0:T(8,128)(2,1)S(1)} collective-permute-done((bf16[128,1024]{1,0:T(8,128)(2,1)S(1)}, bf16[128,1024]{1,0:T(8,128)(2,1)S(1)}, u32[]{:S(2)}, u32[]{:S(2)}) %collective-permute-start.14) | collective-permute-done | bytes 262176 | tf_op jit(solution)/shard_map/ppermute | solution.py:12
  89.4 6.1 %collective-permute-done.12 = bf16[128,1024]{1,0:T(8,128)(2,1)S(1)} collective-permute-done((bf16[128,1024]{1,0:T(8,128)(2,1)S(1)}, bf16[128,1024]{1,0:T(8,128)(2,1)S(1)}, u32[]{:S(2)}, u32[]{:S(2)}) %collective-permute-start.12) | collective-permute-done | bytes 262176 | tf_op jit(solution)/shard_map/ppermute | solution.py:12
  97.4 2.1 %collective-permute-start.16 = (bf16[128,1024]{1,0:T(8,128)(2,1)S(1)}, bf16[128,1024]{1,0:T(8,128)(2,1)S(1)}, u32[]{:S(2)}, u32[]{:S(2)}) collective-permute-start(bf16[128,1024]{1,0:T(8,128)(2,1)S(1)} %fusion.132), channel_id=1, source_target_pairs={{1,0},{2,1},{3,2},{4,3},{5,4},{6,5},{7,6},{9,8},{10,9},{11,10},{12... | collective-permute-start | bytes 786440 | tf_op jit(solution)/shard_map/ppermute | solution.py:12
  100.8 4.3 %collective-permute-done.17 = bf16[128,1024]{1,0:T(8,128)(2,1)S(1)} collective-permute-done((bf16[128,1024]{1,0:T(8,128)(2,1)S(1)}, bf16[128,1024]{1,0:T(8,128)(2,1)S(1)}, u32[]{:S(2)}, u32[]{:S(2)}) %collective-permute-start.17) | collective-permute-done | bytes 262176 | tf_op jit(solution)/shard_map/ppermute | solution.py:12
  105.6 2.4 %collective-permute-done.16 = bf16[128,1024]{1,0:T(8,128)(2,1)S(1)} collective-permute-done((bf16[128,1024]{1,0:T(8,128)(2,1)S(1)}, bf16[128,1024]{1,0:T(8,128)(2,1)S(1)}, u32[]{:S(2)}, u32[]{:S(2)}) %collective-permute-start.16) | collective-permute-done | bytes 262176 | tf_op jit(solution)/shard_map/ppermute | solution.py:12
  108.5 6.0 %collective-permute-done.15 = bf16[128,1024]{1,0:T(8,128)(2,1)S(1)} collective-permute-done((bf16[128,1024]{1,0:T(8,128)(2,1)S(1)}, bf16[128,1024]{1,0:T(8,128)(2,1)S(1)}, u32[]{:S(2)}, u32[]{:S(2)}) %collective-permute-start.15) | collective-permute-done | bytes 262176 | tf_op jit(solution)/shard_map/ppermute | solution.py:12
  116.3 2.3 %collective-permute-start.19 = (bf16[128,1024]{1,0:T(8,128)(2,1)S(1)}, bf16[128,1024]{1,0:T(8,128)(2,1)S(1)}, u32[]{:S(2)}, u32[]{:S(2)}) collective-permute-start(bf16[128,1024]{1,0:T(8,128)(2,1)S(1)} %fusion.129), channel_id=1, source_target_pairs={{1,0},{2,1},{3,2},{4,3},{5,4},{6,5},{7,6},{9,8},{10,9},{11,10},{12... | collective-permute-start | bytes 786440 | tf_op jit(solution)/shard_map/ppermute | solution.py:12
  119.9 3.8 %collective-permute-done.20 = bf16[128,1024]{1,0:T(8,128)(2,1)S(1)} collective-permute-done((bf16[128,1024]{1,0:T(8,128)(2,1)S(1)}, bf16[128,1024]{1,0:T(8,128)(2,1)S(1)}, u32[]{:S(2)}, u32[]{:S(2)}) %collective-permute-start.20) | collective-permute-done | bytes 262176 | tf_op jit(solution)/shard_map/ppermute | solution.py:12
  124.1 2.5 %collective-permute-done.19 = bf16[128,1024]{1,0:T(8,128)(2,1)S(1)} collective-permute-done((bf16[128,1024]{1,0:T(8,128)(2,1)S(1)}, bf16[128,1024]{1,0:T(8,128)(2,1)S(1)}, u32[]{:S(2)}, u32[]{:S(2)}) %collective-permute-start.19) | collective-permute-done | bytes 262176 | tf_op jit(solution)/shard_map/ppermute | solution.py:12
  127.1 6.7 %collective-permute-done.18 = bf16[128,1024]{1,0:T(8,128)(2,1)S(1)} collective-permute-done((bf16[128,1024]{1,0:T(8,128)(2,1)S(1)}, bf16[128,1024]{1,0:T(8,128)(2,1)S(1)}, u32[]{:S(2)}, u32[]{:S(2)}) %collective-permute-start.18) | collective-permute-done | bytes 262176 | tf_op jit(solution)/shard_map/ppermute | solution.py:12
  (43 shorter events, 21.4 us)
Async XLA Ops:
  0.0 20.9 %copy-start = (bf16[1,1,128,1024]{3,2,1,0:T(8,128)(2,1)S(1)}, bf16[1,1,128,1024]{3,2,1,0:T(8,128)(2,1)}, u32[]{:S(2)}) copy-start(bf16[1,1,128,1024]{3,2,1,0:T(8,128)(2,1)} %param.4) | copy-start | bytes 786436
  2.6 10.7 %collective-permute-start.1 = (bf16[128,1024]{1,0:T(8,128)(2,1)S(1)}, bf16[128,1024]{1,0:T(8,128)(2,1)S(1)}, u32[]{:S(2)}, u32[]{:S(2)}) collective-permute-start(bf16[128,1024]{1,0:T(8,128)(2,1)S(1)} %select_convert_fusion), channel_id=1, source_target_pairs={{0,1},{1,2},{2,3},{3,4},{4,5},{5,6},{6,7},{8,9},{9,10},{10,11},{11... | collective-permute-start | bytes 786440 | tf_op jit(solution)/shard_map/ppermute | solution.py:12
  7.1 8.4 %collective-permute-start.2 = (bf16[128,1024]{1,0:T(8,128)(2,1)S(1)}, bf16[128,1024]{1,0:T(8,128)(2,1)S(1)}, u32[]{:S(2)}, u32[]{:S(2)}) collective-permute-start(bf16[128,1024]{1,0:T(8,128)(2,1)S(1)} %select_convert_fusion), channel_id=1, source_target_pairs={{0,9},{1,10},{2,11},{3,12},{4,13},{5,14},{6,15},{7,16},{8,17},{9,1... | collective-permute-start | bytes 786440 | tf_op jit(solution)/shard_map/ppermute | solution.py:12
  10.0 10.9 %collective-permute-start = (bf16[128,1024]{1,0:T(8,128)(2,1)S(1)}, bf16[128,1024]{1,0:T(8,128)(2,1)S(1)}, u32[]{:S(2)}, u32[]{:S(2)}) collective-permute-start(bf16[128,1024]{1,0:T(8,128)(2,1)S(1)} %select_convert_fusion), channel_id=1, source_target_pairs={{0,8},{8,16},{16,24},{1,9},{9,17},{17,25},{2,10},{10,18},{18,26},{... | collective-permute-start | bytes 786440 | tf_op jit(solution)/shard_map/ppermute | solution.py:12
  13.2 7.6 %copy-start.1 = (bf16[1,1,3,1024,1024]{4,3,2,1,0:T(8,128)(2,1)S(1)}, bf16[1,1,3,1024,1024]{4,3,2,1,0:T(8,128)(2,1)}, u32[]{:S(2)}) copy-start(bf16[1,1,3,1024,1024]{4,3,2,1,0:T(8,128)(2,1)} %param.5) | copy-start | bytes 18874372
  21.4 11.3 %collective-permute-start.5 = (bf16[128,1024]{1,0:T(8,128)(2,1)S(1)}, bf16[128,1024]{1,0:T(8,128)(2,1)S(1)}, u32[]{:S(2)}, u32[]{:S(2)}) collective-permute-start(bf16[128,1024]{1,0:T(8,128)(2,1)S(1)} %fusion.144), channel_id=1, source_target_pairs={{0,9},{1,10},{2,11},{3,12},{4,13},{5,14},{6,15},{7,16},{8,17},{9,1... | collective-permute-start | bytes 786440 | tf_op jit(solution)/shard_map/ppermute | solution.py:12
  27.6 5.6 %collective-permute-start.4 = (bf16[128,1024]{1,0:T(8,128)(2,1)S(1)}, bf16[128,1024]{1,0:T(8,128)(2,1)S(1)}, u32[]{:S(2)}, u32[]{:S(2)}) collective-permute-start(bf16[128,1024]{1,0:T(8,128)(2,1)S(1)} %fusion.144), channel_id=1, source_target_pairs={{0,1},{1,2},{2,3},{3,4},{4,5},{5,6},{6,7},{8,9},{9,10},{10,11},{11... | collective-permute-start | bytes 786440 | tf_op jit(solution)/shard_map/ppermute | solution.py:12
  29.5 8.3 %collective-permute-start.3 = (bf16[128,1024]{1,0:T(8,128)(2,1)S(1)}, bf16[128,1024]{1,0:T(8,128)(2,1)S(1)}, u32[]{:S(2)}, u32[]{:S(2)}) collective-permute-start(bf16[128,1024]{1,0:T(8,128)(2,1)S(1)} %fusion.144), channel_id=1, source_target_pairs={{0,8},{8,16},{16,24},{1,9},{9,17},{17,25},{2,10},{10,18},{18,26},{... | collective-permute-start | bytes 786440 | tf_op jit(solution)/shard_map/ppermute | solution.py:12
  38.4 11.5 %collective-permute-start.8 = (bf16[128,1024]{1,0:T(8,128)(2,1)S(1)}, bf16[128,1024]{1,0:T(8,128)(2,1)S(1)}, u32[]{:S(2)}, u32[]{:S(2)}) collective-permute-start(bf16[128,1024]{1,0:T(8,128)(2,1)S(1)} %fusion.141), channel_id=1, source_target_pairs={{0,9},{1,10},{2,11},{3,12},{4,13},{5,14},{6,15},{7,16},{8,17},{9,1... | collective-permute-start | bytes 786440 | tf_op jit(solution)/shard_map/ppermute | solution.py:12
  44.7 5.6 %collective-permute-start.7 = (bf16[128,1024]{1,0:T(8,128)(2,1)S(1)}, bf16[128,1024]{1,0:T(8,128)(2,1)S(1)}, u32[]{:S(2)}, u32[]{:S(2)}) collective-permute-start(bf16[128,1024]{1,0:T(8,128)(2,1)S(1)} %fusion.141), channel_id=1, source_target_pairs={{0,1},{1,2},{2,3},{3,4},{4,5},{5,6},{6,7},{8,9},{9,10},{10,11},{11... | collective-permute-start | bytes 786440 | tf_op jit(solution)/shard_map/ppermute | solution.py:12
  46.6 8.3 %collective-permute-start.6 = (bf16[128,1024]{1,0:T(8,128)(2,1)S(1)}, bf16[128,1024]{1,0:T(8,128)(2,1)S(1)}, u32[]{:S(2)}, u32[]{:S(2)}) collective-permute-start(bf16[128,1024]{1,0:T(8,128)(2,1)S(1)} %fusion.141), channel_id=1, source_target_pairs={{0,8},{8,16},{16,24},{1,9},{9,17},{17,25},{2,10},{10,18},{18,26},{... | collective-permute-start | bytes 786440 | tf_op jit(solution)/shard_map/ppermute | solution.py:12
  55.0 33.5 %slice-start = ((s8[6291456]{0:T(1024)(128)(4,1)}), s8[2097152]{0:T(1024)(128)(4,1)S(1)}, s32[]{:S(2)}) async-start(s8[6291456]{0:T(1024)(128)(4,1)} %bitcast.143), calls=%async_computation | async-start | bytes 4194304
  55.5 8.1 %collective-permute-start.10 = (bf16[128,1024]{1,0:T(8,128)(2,1)S(1)}, bf16[128,1024]{1,0:T(8,128)(2,1)S(1)}, u32[]{:S(2)}, u32[]{:S(2)}) collective-permute-start(bf16[128,1024]{1,0:T(8,128)(2,1)S(1)} %fusion.138), channel_id=1, source_target_pairs={{1,0},{2,1},{3,2},{4,3},{5,4},{6,5},{7,6},{9,8},{10,9},{11,10},{12... | collective-permute-start | bytes 786440 | tf_op jit(solution)/shard_map/ppermute | solution.py:12
  58.9 11.4 %collective-permute-start.11 = (bf16[128,1024]{1,0:T(8,128)(2,1)S(1)}, bf16[128,1024]{1,0:T(8,128)(2,1)S(1)}, u32[]{:S(2)}, u32[]{:S(2)}) collective-permute-start(bf16[128,1024]{1,0:T(8,128)(2,1)S(1)} %fusion.138), channel_id=1, source_target_pairs={{9,0},{10,1},{11,2},{12,3},{13,4},{14,5},{15,6},{16,7},{17,8},{18,... | collective-permute-start | bytes 786440 | tf_op jit(solution)/shard_map/ppermute | solution.py:12
  60.2 14.7 %collective-permute-start.9 = (bf16[128,1024]{1,0:T(8,128)(2,1)S(1)}, bf16[128,1024]{1,0:T(8,128)(2,1)S(1)}, u32[]{:S(2)}, u32[]{:S(2)}) collective-permute-start(bf16[128,1024]{1,0:T(8,128)(2,1)S(1)} %fusion.138), channel_id=1, source_target_pairs={{8,0},{16,8},{24,16},{9,1},{17,9},{25,17},{10,2},{18,10},{26,18},{... | collective-permute-start | bytes 786440 | tf_op jit(solution)/shard_map/ppermute | solution.py:12
  65.6 22.9 %slice-start.1 = ((s8[6291456]{0:T(1024)(128)(4,1)}), s8[4194304]{0:T(1024)(128)(4,1)S(1)}, s32[]{:S(2)}) async-start(s8[6291456]{0:T(1024)(128)(4,1)} %bitcast.143), calls=%async_computation.1 | async-start | bytes 8388608
  77.0 11.5 %collective-permute-start.14 = (bf16[128,1024]{1,0:T(8,128)(2,1)S(1)}, bf16[128,1024]{1,0:T(8,128)(2,1)S(1)}, u32[]{:S(2)}, u32[]{:S(2)}) collective-permute-start(bf16[128,1024]{1,0:T(8,128)(2,1)S(1)} %fusion.135), channel_id=1, source_target_pairs={{9,0},{10,1},{11,2},{12,3},{13,4},{14,5},{15,6},{16,7},{17,8},{18,... | collective-permute-start | bytes 786440 | tf_op jit(solution)/shard_map/ppermute | solution.py:12
  78.3 10.6 %collective-permute-start.13 = (bf16[128,1024]{1,0:T(8,128)(2,1)S(1)}, bf16[128,1024]{1,0:T(8,128)(2,1)S(1)}, u32[]{:S(2)}, u32[]{:S(2)}) collective-permute-start(bf16[128,1024]{1,0:T(8,128)(2,1)S(1)} %fusion.135), channel_id=1, source_target_pairs={{1,0},{2,1},{3,2},{4,3},{5,4},{6,5},{7,6},{9,8},{10,9},{11,10},{12... | collective-permute-start | bytes 786440 | tf_op jit(solution)/shard_map/ppermute | solution.py:12
  80.3 15.3 %collective-permute-start.12 = (bf16[128,1024]{1,0:T(8,128)(2,1)S(1)}, bf16[128,1024]{1,0:T(8,128)(2,1)S(1)}, u32[]{:S(2)}, u32[]{:S(2)}) collective-permute-start(bf16[128,1024]{1,0:T(8,128)(2,1)S(1)} %fusion.135), channel_id=1, source_target_pairs={{8,0},{16,8},{24,16},{9,1},{17,9},{25,17},{10,2},{18,10},{26,18},{... | collective-permute-start | bytes 786440 | tf_op jit(solution)/shard_map/ppermute | solution.py:12
  96.1 9.0 %collective-permute-start.17 = (bf16[128,1024]{1,0:T(8,128)(2,1)S(1)}, bf16[128,1024]{1,0:T(8,128)(2,1)S(1)}, u32[]{:S(2)}, u32[]{:S(2)}) collective-permute-start(bf16[128,1024]{1,0:T(8,128)(2,1)S(1)} %fusion.132), channel_id=1, source_target_pairs={{9,0},{10,1},{11,2},{12,3},{13,4},{14,5},{15,6},{16,7},{17,8},{18,... | collective-permute-start | bytes 786440 | tf_op jit(solution)/shard_map/ppermute | solution.py:12
  97.4 10.6 %collective-permute-start.16 = (bf16[128,1024]{1,0:T(8,128)(2,1)S(1)}, bf16[128,1024]{1,0:T(8,128)(2,1)S(1)}, u32[]{:S(2)}, u32[]{:S(2)}) collective-permute-start(bf16[128,1024]{1,0:T(8,128)(2,1)S(1)} %fusion.132), channel_id=1, source_target_pairs={{1,0},{2,1},{3,2},{4,3},{5,4},{6,5},{7,6},{9,8},{10,9},{11,10},{12... | collective-permute-start | bytes 786440 | tf_op jit(solution)/shard_map/ppermute | solution.py:12
  99.5 14.9 %collective-permute-start.15 = (bf16[128,1024]{1,0:T(8,128)(2,1)S(1)}, bf16[128,1024]{1,0:T(8,128)(2,1)S(1)}, u32[]{:S(2)}, u32[]{:S(2)}) collective-permute-start(bf16[128,1024]{1,0:T(8,128)(2,1)S(1)} %fusion.132), channel_id=1, source_target_pairs={{8,0},{16,8},{24,16},{9,1},{17,9},{25,17},{10,2},{18,10},{26,18},{... | collective-permute-start | bytes 786440 | tf_op jit(solution)/shard_map/ppermute | solution.py:12
  115.0 8.7 %collective-permute-start.20 = (bf16[128,1024]{1,0:T(8,128)(2,1)S(1)}, bf16[128,1024]{1,0:T(8,128)(2,1)S(1)}, u32[]{:S(2)}, u32[]{:S(2)}) collective-permute-start(bf16[128,1024]{1,0:T(8,128)(2,1)S(1)} %fusion.129), channel_id=1, source_target_pairs={{9,0},{10,1},{11,2},{12,3},{13,4},{14,5},{15,6},{16,7},{17,8},{18,... | collective-permute-start | bytes 786440 | tf_op jit(solution)/shard_map/ppermute | solution.py:12
  116.3 10.4 %collective-permute-start.19 = (bf16[128,1024]{1,0:T(8,128)(2,1)S(1)}, bf16[128,1024]{1,0:T(8,128)(2,1)S(1)}, u32[]{:S(2)}, u32[]{:S(2)}) collective-permute-start(bf16[128,1024]{1,0:T(8,128)(2,1)S(1)} %fusion.129), channel_id=1, source_target_pairs={{1,0},{2,1},{3,2},{4,3},{5,4},{6,5},{7,6},{9,8},{10,9},{11,10},{12... | collective-permute-start | bytes 786440 | tf_op jit(solution)/shard_map/ppermute | solution.py:12
  118.6 15.3 %collective-permute-start.18 = (bf16[128,1024]{1,0:T(8,128)(2,1)S(1)}, bf16[128,1024]{1,0:T(8,128)(2,1)S(1)}, u32[]{:S(2)}, u32[]{:S(2)}) collective-permute-start(bf16[128,1024]{1,0:T(8,128)(2,1)S(1)} %fusion.129), channel_id=1, source_target_pairs={{8,0},{16,8},{24,16},{9,1},{17,9},{25,17},{10,2},{18,10},{26,18},{... | collective-permute-start | bytes 786440 | tf_op jit(solution)/shard_map/ppermute | solution.py:12
where the time goes:
time: 136 us; the launch traced here: 135 us
  waiting for transfers between devices  59.6 us (44%)
  starting transfers between devices  53.4 us (39%)
  matrix products  19.1 us (14%)
  other arithmetic  2.54 us (2%)
    ppermute x21, waiting for transfers between devices, passed_along(): return lax.ppermute(block, axis, route)  59.6 us
    ppermute x21, starting transfers between devices, passed_along(): return lax.ppermute(block, axis, route)  53.4 us
    dot_general x7, matrix products, body(): jnp.dot(diagonal_in, operator_set[2], preferred_element_type=jnp.float32)  6.56 us
    dot_general x7, matrix products, body(): jnp.dot(from_col, operator_set[1], preferred_element_type=jnp.float32)  6.47 us
    dot_general x7, matrix products, body(): jnp.dot(from_row, operator_set[0], preferred_element_type=jnp.float32)  6.05 us
  transfers between devices with their start and end apart: 21, of which 14 were waited for; matrix products, arithmetic and copies ran while one was open for 10% of the time, Pallas kernels for 0%

commit v1 on v0

v1 whole, which is shorter than its diff:
```python
import jax
import jax.numpy as jnp
from jax import lax
from jax.sharding import PartitionSpec as P

TICKS = 8
AXES = ("row", "col")


def closed(route, rows, cols):
    every = [(r, c) for r in range(rows) for c in range(cols)]
    sources, targets = {a for a, _ in route}, {b for _, b in route}
    free = [p for p in every if p not in targets]
    for a in [p for p in every if p not in sources]:
        far = lambda b: (b == a, abs(b[0] - a[0]) + abs(b[1] // 2 - a[1] // 2), b[1] != a[1])
        b = min(free, key=far)
        free.remove(b)
        route = route + [(a, b)]
    return [(a[0] * cols + a[1], b[0] * cols + b[1]) for a, b in route if a != b]


def shift(block, dr, dc):
    rows, cols = lax.axis_size("row"), lax.axis_size("col")
    inside = lambda r, c: 0 <= r < rows and 0 <= c < cols
    every = [(r, c) for r in range(rows) for c in range(cols)]
    route = [((r, c), (r + dr, c + dc)) for r, c in every if inside(r + dr, c + dc)]
    return lax.ppermute(block, AXES, closed(route, rows, cols))


def body(rhs, operators, positions, start_tick):
    rows, cols = lax.axis_size("row"), lax.axis_size("col")
    batches, width = rhs.shape[2:]
    ops = operators[0, 0]
    i, j = lax.axis_index("row"), lax.axis_index("col")
    local_point = positions - (i * cols + j) * width
    column_ids = lax.broadcasted_iota(jnp.int32, (batches, width), 1)
    spike = (local_point[:, None] == column_ids).astype(jnp.float32)
    source = rhs[0, 0].astype(jnp.float32) + 4.0 * spike
    traces = jnp.where((0 >= start_tick)[:, None], source, 0.0).astype(jnp.bfloat16)
    turning = TICKS // 2
    for tick in range(1, TICKS):
        s = 1 if tick < turning else -1
        has_row = (i - s >= 0) & (i - s < rows)
        has_col = (j - s >= 0) & (j - s < cols)
        begun = start_tick < tick
        keep = lambda x, ok: jnp.where((begun & ok)[:, None], x, jnp.zeros_like(x))
        up = shift(traces, s, 0)
        left = shift(traces, 0, s)
        up, left = keep(up, has_row), keep(left, has_col)
        corner = keep(shift(up, 0, s), has_col)
        summed = source
        for mat, block in enumerate((up, left, corner)):
            summed = summed + jnp.dot(block, ops[mat], preferred_element_type=jnp.float32)
        running = (tick >= start_tick)[:, None]
        traces = jnp.where(running, summed, 0.0).astype(jnp.bfloat16)
    return traces[None, None]


def solution(mesh):
    placed = (P("row", "col", None, None), P("row", "col", None, None, None), P(), P())
    return jax.shard_map(
        body, mesh=mesh, in_specs=placed, out_specs=P("row", "col", None, None), check_vma=False
    )
```

time: 136 us -> 118 us (0.87)
  starting transfers between devices: 53.4 us -> 36.4 us
  matrix products: 19.1 us -> 14.9 us
  waiting for transfers between devices: 59.6 us -> 62.9 us
    ppermute x21, starting transfers between devices: 53.4 us -> 36.4 us  [shift(): return lax.ppermute(block, AXES, closed(route, rows, cols))]
    dot_general x21, matrix products: 19.1 us -> 14.9 us  [body(): jnp.dot(block, ops[mat], preferred_element_type=jnp.float32)]
    ppermute x21, waiting for transfers between devices: 59.6 us -> 62.9 us  [shift(): return lax.ppermute(block, AXES, closed(route, rows, cols))]
  transfers between devices with their start and end apart: 21 -> 21, of which waited for: 14 -> 15; matrix products, arithmetic and copies ran while one was open for 10% -> 5% of each run, Pallas kernels for 0% -> 0%
where the time goes in v1:
time: 118 us
  waiting for transfers between devices  62.9 us (53%)
  starting transfers between devices  36.4 us (31%)
  matrix products  14.9 us (13%)
  other arithmetic  3.69 us (3%)
    ppermute x21, waiting for transfers between devices, shift(): return lax.ppermute(block, AXES, closed(route, rows, cols))  62.9 us
    ppermute x21, starting transfers between devices, shift(): return lax.ppermute(block, AXES, closed(route, rows, cols))  36.4 us
    dot_general x21, matrix products, body(): jnp.dot(block, ops[mat], preferred_element_type=jnp.float32)  14.9 us
  transfers between devices with their start and end apart: 21, of which 15 were waited for; matrix products, arithmetic and copies ran while one was open for 5% of the time, Pallas kernels for 0%

profile of v1, /device:TPU:1, one launch (start us, length us, event | category | flops | bytes accessed | tf_op | source)
XLA Modules:
  0.0 118.1 jit_solution(11342453892487205974)
XLA Ops:
  0.0 0.8 broadcast_subtract_fusion
  0.8 1.0 broadcast_compare_fusion.7
  1.8 1.2 %select_convert_fusion = bf16[128,1024]{1,0:T(8,128)(2,1)S(1)} fusion(bf16[1,1,128,1024]{3,2,1,0:T(8,128)(2,1)} %param.4, s32[128]{0:T(128)S(1)} %broadcast_subtract_fusion, pred[128]{0:T(512)(128)(4,1)S(1)} %get-tuple-element.25), kind=kLoop, calls=%fused_computation.100 | loop fusion | flops 786432 | bytes 524928 | tf_op jit(solution)/shard_map/convert_element_type | solution.py:39
  3.1 2.2 %collective-permute-start = (bf16[128,1024]{1,0:T(8,128)(2,1)S(1)}, bf16[128,1024]{1,0:T(8,128)(2,1)S(1)}, u32[]{:S(2)}, u32[]{:S(2)}) collective-permute-start(bf16[128,1024]{1,0:T(8,128)(2,1)S(1)} %select_convert_fusion), channel_id=1, source_target_pairs={{0,8},{1,9},{2,10},{3,11},{4,12},{5,13},{6,14},{7,15},{8,16},{9,17... | collective-permute-start | bytes 786440 | tf_op jit(solution)/shard_map/ppermute | solution.py:27
  5.3 2.1 %collective-permute-start.1 = (bf16[128,1024]{1,0:T(8,128)(2,1)S(1)}, bf16[128,1024]{1,0:T(8,128)(2,1)S(1)}, u32[]{:S(2)}, u32[]{:S(2)}) collective-permute-start(bf16[128,1024]{1,0:T(8,128)(2,1)S(1)} %select_convert_fusion), channel_id=1, source_target_pairs={{0,1},{1,2},{2,3},{3,4},{4,5},{5,6},{6,7},{8,9},{9,10},{10,11},{11... | collective-permute-start | bytes 786440 | tf_op jit(solution)/shard_map/ppermute | solution.py:27
  7.3 6.0 %collective-permute-done = bf16[128,1024]{1,0:T(8,128)(2,1)S(1)} collective-permute-done((bf16[128,1024]{1,0:T(8,128)(2,1)S(1)}, bf16[128,1024]{1,0:T(8,128)(2,1)S(1)}, u32[]{:S(2)}, u32[]{:S(2)}) %collective-permute-start) | collective-permute-done | bytes 262176 | tf_op jit(solution)/shard_map/ppermute | solution.py:27
  13.4 2.4 %collective-permute-start.2 = (bf16[128,1024]{1,0:T(8,128)(2,1)S(1)}, bf16[128,1024]{1,0:T(8,128)(2,1)S(1)}, u32[]{:S(2)}, u32[]{:S(2)}) collective-permute-start(bf16[128,1024]{1,0:T(8,128)(2,1)S(1)} %broadcast_select_fusion), channel_id=1, source_target_pairs={{0,1},{1,2},{2,3},{3,4},{4,5},{5,6},{6,7},{8,9},{9,10},{10,11},{11... | collective-permute-start | bytes 786440 | tf_op jit(solution)/shard_map/ppermute | solution.py:27
  15.8 2.1 %fusion.26 = f32[128,1024]{1,0:T(8,128)S(1)} fusion(bf16[1,1,3,1024,1024]{4,3,2,1,0:T(8,128)(2,1)} %param.5, bf16[128,1024]{1,0:T(8,128)(2,1)S(1)} %collective-permute-done.1, pred[128]{0:T(512)(128)(4,1)S(1)} %get-tuple-element.12), kind=kOutput, calls=%fused_computation.26 | convolution fusion | flops 268566528 | bytes 2883712 | tf_op jit(solution)/shard_map/dot_general | solution.py:53
  17.9 1.2 %collective-permute-done.2 = bf16[128,1024]{1,0:T(8,128)(2,1)S(1)} collective-permute-done((bf16[128,1024]{1,0:T(8,128)(2,1)S(1)}, bf16[128,1024]{1,0:T(8,128)(2,1)S(1)}, u32[]{:S(2)}, u32[]{:S(2)}) %collective-permute-start.2) | collective-permute-done | bytes 262176 | tf_op jit(solution)/shard_map/ppermute | solution.py:27
  19.1 2.1 %fusion.12 = f32[128,1024]{1,0:T(8,128)S(1)} fusion(bf16[1,1,3,1024,1024]{4,3,2,1,0:T(8,128)(2,1)} %param.5, bf16[128,1024]{1,0:T(8,128)(2,1)S(1)} %collective-permute-done.2, pred[128]{0:T(512)(128)(4,1)S(1)} %get-tuple-element.12), kind=kOutput, calls=%fused_computation.12 | convolution fusion | flops 268566528 | bytes 2883712 | tf_op jit(solution)/shard_map/dot_general | solution.py:53
  21.9 2.5 %collective-permute-start.4 = (bf16[128,1024]{1,0:T(8,128)(2,1)S(1)}, bf16[128,1024]{1,0:T(8,128)(2,1)S(1)}, u32[]{:S(2)}, u32[]{:S(2)}) collective-permute-start(bf16[128,1024]{1,0:T(8,128)(2,1)S(1)} %fusion.144), channel_id=1, source_target_pairs={{0,1},{1,2},{2,3},{3,4},{4,5},{5,6},{6,7},{8,9},{9,10},{10,11},{11... | collective-permute-start | bytes 786440 | tf_op jit(solution)/shard_map/ppermute | solution.py:27
  24.4 4.8 %collective-permute-done.3 = bf16[128,1024]{1,0:T(8,128)(2,1)S(1)} collective-permute-done((bf16[128,1024]{1,0:T(8,128)(2,1)S(1)}, bf16[128,1024]{1,0:T(8,128)(2,1)S(1)}, u32[]{:S(2)}, u32[]{:S(2)}) %collective-permute-start.3) | collective-permute-done | bytes 262176 | tf_op jit(solution)/shard_map/ppermute | solution.py:27
  29.3 4.3 %collective-permute-start.5 = (bf16[128,1024]{1,0:T(8,128)(2,1)S(1)}, bf16[128,1024]{1,0:T(8,128)(2,1)S(1)}, u32[]{:S(2)}, u32[]{:S(2)}) collective-permute-start(bf16[128,1024]{1,0:T(8,128)(2,1)S(1)} %broadcast_select_fusion.1), channel_id=1, source_target_pairs={{0,1},{1,2},{2,3},{3,4},{4,5},{5,6},{6,7},{8,9},{9,10},{10,11},{11... | collective-permute-start | bytes 786440 | tf_op jit(solution)/shard_map/ppermute | solution.py:27
  34.1 2.8 %collective-permute-done.5 = bf16[128,1024]{1,0:T(8,128)(2,1)S(1)} collective-permute-done((bf16[128,1024]{1,0:T(8,128)(2,1)S(1)}, bf16[128,1024]{1,0:T(8,128)(2,1)S(1)}, u32[]{:S(2)}, u32[]{:S(2)}) %collective-permute-start.5) | collective-permute-done | bytes 262176 | tf_op jit(solution)/shard_map/ppermute | solution.py:27
  38.1 2.6 %collective-permute-start.7 = (bf16[128,1024]{1,0:T(8,128)(2,1)S(1)}, bf16[128,1024]{1,0:T(8,128)(2,1)S(1)}, u32[]{:S(2)}, u32[]{:S(2)}) collective-permute-start(bf16[128,1024]{1,0:T(8,128)(2,1)S(1)} %fusion.141), channel_id=1, source_target_pairs={{0,1},{1,2},{2,3},{3,4},{4,5},{5,6},{6,7},{8,9},{9,10},{10,11},{11... | collective-permute-start | bytes 786440 | tf_op jit(solution)/shard_map/ppermute | solution.py:27
  40.6 4.8 %collective-permute-done.6 = bf16[128,1024]{1,0:T(8,128)(2,1)S(1)} collective-permute-done((bf16[128,1024]{1,0:T(8,128)(2,1)S(1)}, bf16[128,1024]{1,0:T(8,128)(2,1)S(1)}, u32[]{:S(2)}, u32[]{:S(2)}) %collective-permute-start.6) | collective-permute-done | bytes 262176 | tf_op jit(solution)/shard_map/ppermute | solution.py:27
  45.5 4.3 %collective-permute-start.8 = (bf16[128,1024]{1,0:T(8,128)(2,1)S(1)}, bf16[128,1024]{1,0:T(8,128)(2,1)S(1)}, u32[]{:S(2)}, u32[]{:S(2)}) collective-permute-start(bf16[128,1024]{1,0:T(8,128)(2,1)S(1)} %broadcast_select_fusion.2), channel_id=1, source_target_pairs={{0,1},{1,2},{2,3},{3,4},{4,5},{5,6},{6,7},{8,9},{9,10},{10,11},{11... | collective-permute-start | bytes 786440 | tf_op jit(solution)/shard_map/ppermute | solution.py:27
  50.3 2.8 %collective-permute-done.8 = bf16[128,1024]{1,0:T(8,128)(2,1)S(1)} collective-permute-done((bf16[128,1024]{1,0:T(8,128)(2,1)S(1)}, bf16[128,1024]{1,0:T(8,128)(2,1)S(1)}, u32[]{:S(2)}, u32[]{:S(2)}) %collective-permute-start.8) | collective-permute-done | bytes 262176 | tf_op jit(solution)/shard_map/ppermute | solution.py:27
  54.3 2.3 %collective-permute-start.10 = (bf16[128,1024]{1,0:T(8,128)(2,1)S(1)}, bf16[128,1024]{1,0:T(8,128)(2,1)S(1)}, u32[]{:S(2)}, u32[]{:S(2)}) collective-permute-start(bf16[128,1024]{1,0:T(8,128)(2,1)S(1)} %fusion.138), channel_id=1, source_target_pairs={{1,0},{2,1},{3,2},{4,3},{5,4},{6,5},{7,6},{9,8},{10,9},{11,10},{12... | collective-permute-start | bytes 786440 | tf_op jit(solution)/shard_map/ppermute | solution.py:27
  56.6 3.2 %collective-permute-done.9 = bf16[128,1024]{1,0:T(8,128)(2,1)S(1)} collective-permute-done((bf16[128,1024]{1,0:T(8,128)(2,1)S(1)}, bf16[128,1024]{1,0:T(8,128)(2,1)S(1)}, u32[]{:S(2)}, u32[]{:S(2)}) %collective-permute-start.9) | collective-permute-done | bytes 262176 | tf_op jit(solution)/shard_map/ppermute | solution.py:27
  59.9 3.2 %collective-permute-start.11 = (bf16[128,1024]{1,0:T(8,128)(2,1)S(1)}, bf16[128,1024]{1,0:T(8,128)(2,1)S(1)}, u32[]{:S(2)}, u32[]{:S(2)}) collective-permute-start(bf16[128,1024]{1,0:T(8,128)(2,1)S(1)} %broadcast_select_fusion.3), channel_id=1, source_target_pairs={{1,0},{2,1},{3,2},{4,3},{5,4},{6,5},{7,6},{9,8},{10,9},{11,10},{12... | collective-permute-start | bytes 786440 | tf_op jit(solution)/shard_map/ppermute | solution.py:27
  63.7 4.5 %collective-permute-done.11 = bf16[128,1024]{1,0:T(8,128)(2,1)S(1)} collective-permute-done((bf16[128,1024]{1,0:T(8,128)(2,1)S(1)}, bf16[128,1024]{1,0:T(8,128)(2,1)S(1)}, u32[]{:S(2)}, u32[]{:S(2)}) %collective-permute-start.11) | collective-permute-done | bytes 262176 | tf_op jit(solution)/shard_map/ppermute | solution.py:27
  69.3 1.9 %collective-permute-start.12 = (bf16[128,1024]{1,0:T(8,128)(2,1)S(1)}, bf16[128,1024]{1,0:T(8,128)(2,1)S(1)}, u32[]{:S(2)}, u32[]{:S(2)}) collective-permute-start(bf16[128,1024]{1,0:T(8,128)(2,1)S(1)} %fusion.135), channel_id=1, source_target_pairs={{8,0},{9,1},{10,2},{11,3},{12,4},{13,5},{14,6},{15,7},{16,8},{17,9... | collective-permute-start | bytes 786440 | tf_op jit(solution)/shard_map/ppermute | solution.py:27
  71.1 5.5 %collective-permute-done.12 = bf16[128,1024]{1,0:T(8,128)(2,1)S(1)} collective-permute-done((bf16[128,1024]{1,0:T(8,128)(2,1)S(1)}, bf16[128,1024]{1,0:T(8,128)(2,1)S(1)}, u32[]{:S(2)}, u32[]{:S(2)}) %collective-permute-start.12) | collective-permute-done | bytes 262176 | tf_op jit(solution)/shard_map/ppermute | solution.py:27
  77.4 5.2 %collective-permute-done.14 = bf16[128,1024]{1,0:T(8,128)(2,1)S(1)} collective-permute-done((bf16[128,1024]{1,0:T(8,128)(2,1)S(1)}, bf16[128,1024]{1,0:T(8,128)(2,1)S(1)}, u32[]{:S(2)}, u32[]{:S(2)}) %collective-permute-start.14) | collective-permute-done | bytes 262176 | tf_op jit(solution)/shard_map/ppermute | solution.py:27
  83.7 3.6 %collective-permute-start.15 = (bf16[128,1024]{1,0:T(8,128)(2,1)S(1)}, bf16[128,1024]{1,0:T(8,128)(2,1)S(1)}, u32[]{:S(2)}, u32[]{:S(2)}) collective-permute-start(bf16[128,1024]{1,0:T(8,128)(2,1)S(1)} %fusion.132), channel_id=1, source_target_pairs={{8,0},{9,1},{10,2},{11,3},{12,4},{13,5},{14,6},{15,7},{16,8},{17,9... | collective-permute-start | bytes 786440 | tf_op jit(solution)/shard_map/ppermute | solution.py:27
  87.3 6.0 %collective-permute-done.15 = bf16[128,1024]{1,0:T(8,128)(2,1)S(1)} collective-permute-done((bf16[128,1024]{1,0:T(8,128)(2,1)S(1)}, bf16[128,1024]{1,0:T(8,128)(2,1)S(1)}, u32[]{:S(2)}, u32[]{:S(2)}) %collective-permute-start.15) | collective-permute-done | bytes 262176 | tf_op jit(solution)/shard_map/ppermute | solution.py:27
  94.5 4.8 %collective-permute-done.17 = bf16[128,1024]{1,0:T(8,128)(2,1)S(1)} collective-permute-done((bf16[128,1024]{1,0:T(8,128)(2,1)S(1)}, bf16[128,1024]{1,0:T(8,128)(2,1)S(1)}, u32[]{:S(2)}, u32[]{:S(2)}) %collective-permute-start.17) | collective-permute-done | bytes 262176 | tf_op jit(solution)/shard_map/ppermute | solution.py:27
  100.4 4.0 %collective-permute-start.18 = (bf16[128,1024]{1,0:T(8,128)(2,1)S(1)}, bf16[128,1024]{1,0:T(8,128)(2,1)S(1)}, u32[]{:S(2)}, u32[]{:S(2)}) collective-permute-start(bf16[128,1024]{1,0:T(8,128)(2,1)S(1)} %fusion.129), channel_id=1, source_target_pairs={{8,0},{9,1},{10,2},{11,3},{12,4},{13,5},{14,6},{15,7},{16,8},{17,9... | collective-permute-start | bytes 786440 | tf_op jit(solution)/shard_map/ppermute | solution.py:27
  104.5 5.9 %collective-permute-done.18 = bf16[128,1024]{1,0:T(8,128)(2,1)S(1)} collective-permute-done((bf16[128,1024]{1,0:T(8,128)(2,1)S(1)}, bf16[128,1024]{1,0:T(8,128)(2,1)S(1)}, u32[]{:S(2)}, u32[]{:S(2)}) %collective-permute-start.18) | collective-permute-done | bytes 262176 | tf_op jit(solution)/shard_map/ppermute | solution.py:27
  111.3 5.1 %collective-permute-done.20 = bf16[128,1024]{1,0:T(8,128)(2,1)S(1)} collective-permute-done((bf16[128,1024]{1,0:T(8,128)(2,1)S(1)}, bf16[128,1024]{1,0:T(8,128)(2,1)S(1)}, u32[]{:S(2)}, u32[]{:S(2)}) %collective-permute-start.20) | collective-permute-done | bytes 262176 | tf_op jit(solution)/shard_map/ppermute | solution.py:27
  116.8 1.3 %fusion.147 = bf16[1,1,128,1024]{3,2,1,0:T(8,128)(2,1)} fusion(f32[128,1024]{1,0:T(8,128)S(1)} %fusion, f32[128,1024]{1,0:T(8,128)S(1)} %fusion.14, bf16[128,1024]{1,0:T(8,128)(2,1)S(1)} %broadcast_select_fusion.6, bf16[1,1,3,1024,1024]{4,3,2,1,0:T(8,128)(2,1)S(1)} %copy-done.1, bf16[1,1,128,1024]{3,2,1,0:T(8,128)(2,1)S(1)} %copy-done, ...), kind=kOutput, calls=%fused_computation.77 | convolution fusion | flops 269615104 | bytes 3933184 | tf_op jit(solution)/shard_map/dot_general | solution.py:53
  (45 shorter events, 11.2 us)
Async XLA Ops:
  0.0 21.2 %copy-start = (bf16[1,1,128,1024]{3,2,1,0:T(8,128)(2,1)S(1)}, bf16[1,1,128,1024]{3,2,1,0:T(8,128)(2,1)}, u32[]{:S(2)}) copy-start(bf16[1,1,128,1024]{3,2,1,0:T(8,128)(2,1)} %param.4) | copy-start | bytes 786436
  0.0 21.2 %copy-start.1 = (bf16[1,1,3,1024,1024]{4,3,2,1,0:T(8,128)(2,1)S(1)}, bf16[1,1,3,1024,1024]{4,3,2,1,0:T(8,128)(2,1)}, u32[]{:S(2)}) copy-start(bf16[1,1,3,1024,1024]{4,3,2,1,0:T(8,128)(2,1)} %param.5) | copy-start | bytes 18874372
  3.1 10.2 %collective-permute-start = (bf16[128,1024]{1,0:T(8,128)(2,1)S(1)}, bf16[128,1024]{1,0:T(8,128)(2,1)S(1)}, u32[]{:S(2)}, u32[]{:S(2)}) collective-permute-start(bf16[128,1024]{1,0:T(8,128)(2,1)S(1)} %select_convert_fusion), channel_id=1, source_target_pairs={{0,8},{1,9},{2,10},{3,11},{4,12},{5,13},{6,14},{7,15},{8,16},{9,17... | collective-permute-start | bytes 786440 | tf_op jit(solution)/shard_map/ppermute | solution.py:27
  5.3 10.5 %collective-permute-start.1 = (bf16[128,1024]{1,0:T(8,128)(2,1)S(1)}, bf16[128,1024]{1,0:T(8,128)(2,1)S(1)}, u32[]{:S(2)}, u32[]{:S(2)}) collective-permute-start(bf16[128,1024]{1,0:T(8,128)(2,1)S(1)} %select_convert_fusion), channel_id=1, source_target_pairs={{0,1},{1,2},{2,3},{3,4},{4,5},{5,6},{6,7},{8,9},{9,10},{10,11},{11... | collective-permute-start | bytes 786440 | tf_op jit(solution)/shard_map/ppermute | solution.py:27
  13.4 5.7 %collective-permute-start.2 = (bf16[128,1024]{1,0:T(8,128)(2,1)S(1)}, bf16[128,1024]{1,0:T(8,128)(2,1)S(1)}, u32[]{:S(2)}, u32[]{:S(2)}) collective-permute-start(bf16[128,1024]{1,0:T(8,128)(2,1)S(1)} %broadcast_select_fusion), channel_id=1, source_target_pairs={{0,1},{1,2},{2,3},{3,4},{4,5},{5,6},{6,7},{8,9},{9,10},{10,11},{11... | collective-permute-start | bytes 786440 | tf_op jit(solution)/shard_map/ppermute | solution.py:27
  21.8 7.4 %collective-permute-start.3 = (bf16[128,1024]{1,0:T(8,128)(2,1)S(1)}, bf16[128,1024]{1,0:T(8,128)(2,1)S(1)}, u32[]{:S(2)}, u32[]{:S(2)}) collective-permute-start(bf16[128,1024]{1,0:T(8,128)(2,1)S(1)} %fusion.144), channel_id=1, source_target_pairs={{0,8},{1,9},{2,10},{3,11},{4,12},{5,13},{6,14},{7,15},{8,16},{9,17... | collective-permute-start | bytes 786440 | tf_op jit(solution)/shard_map/ppermute | solution.py:27
  21.9 11.7 %collective-permute-start.4 = (bf16[128,1024]{1,0:T(8,128)(2,1)S(1)}, bf16[128,1024]{1,0:T(8,128)(2,1)S(1)}, u32[]{:S(2)}, u32[]{:S(2)}) collective-permute-start(bf16[128,1024]{1,0:T(8,128)(2,1)S(1)} %fusion.144), channel_id=1, source_target_pairs={{0,1},{1,2},{2,3},{3,4},{4,5},{5,6},{6,7},{8,9},{9,10},{10,11},{11... | collective-permute-start | bytes 786440 | tf_op jit(solution)/shard_map/ppermute | solution.py:27
  29.3 7.6 %collective-permute-start.5 = (bf16[128,1024]{1,0:T(8,128)(2,1)S(1)}, bf16[128,1024]{1,0:T(8,128)(2,1)S(1)}, u32[]{:S(2)}, u32[]{:S(2)}) collective-permute-start(bf16[128,1024]{1,0:T(8,128)(2,1)S(1)} %broadcast_select_fusion.1), channel_id=1, source_target_pairs={{0,1},{1,2},{2,3},{3,4},{4,5},{5,6},{6,7},{8,9},{9,10},{10,11},{11... | collective-permute-start | bytes 786440 | tf_op jit(solution)/shard_map/ppermute | solution.py:27
  38.0 7.4 %collective-permute-start.6 = (bf16[128,1024]{1,0:T(8,128)(2,1)S(1)}, bf16[128,1024]{1,0:T(8,128)(2,1)S(1)}, u32[]{:S(2)}, u32[]{:S(2)}) collective-permute-start(bf16[128,1024]{1,0:T(8,128)(2,1)S(1)} %fusion.141), channel_id=1, source_target_pairs={{0,8},{1,9},{2,10},{3,11},{4,12},{5,13},{6,14},{7,15},{8,16},{9,17... | collective-permute-start | bytes 786440 | tf_op jit(solution)/shard_map/ppermute | solution.py:27
  38.1 11.7 %collective-permute-start.7 = (bf16[128,1024]{1,0:T(8,128)(2,1)S(1)}, bf16[128,1024]{1,0:T(8,128)(2,1)S(1)}, u32[]{:S(2)}, u32[]{:S(2)}) collective-permute-start(bf16[128,1024]{1,0:T(8,128)(2,1)S(1)} %fusion.141), channel_id=1, source_target_pairs={{0,1},{1,2},{2,3},{3,4},{4,5},{5,6},{6,7},{8,9},{9,10},{10,11},{11... | collective-permute-start | bytes 786440 | tf_op jit(solution)/shard_map/ppermute | solution.py:27
  45.5 7.6 %collective-permute-start.8 = (bf16[128,1024]{1,0:T(8,128)(2,1)S(1)}, bf16[128,1024]{1,0:T(8,128)(2,1)S(1)}, u32[]{:S(2)}, u32[]{:S(2)}) collective-permute-start(bf16[128,1024]{1,0:T(8,128)(2,1)S(1)} %broadcast_select_fusion.2), channel_id=1, source_target_pairs={{0,1},{1,2},{2,3},{3,4},{4,5},{5,6},{6,7},{8,9},{9,10},{10,11},{11... | collective-permute-start | bytes 786440 | tf_op jit(solution)/shard_map/ppermute | solution.py:27
  54.2 5.6 %collective-permute-start.9 = (bf16[128,1024]{1,0:T(8,128)(2,1)S(1)}, bf16[128,1024]{1,0:T(8,128)(2,1)S(1)}, u32[]{:S(2)}, u32[]{:S(2)}) collective-permute-start(bf16[128,1024]{1,0:T(8,128)(2,1)S(1)} %fusion.138), channel_id=1, source_target_pairs={{8,0},{9,1},{10,2},{11,3},{12,4},{13,5},{14,6},{15,7},{16,8},{17,9... | collective-permute-start | bytes 786440 | tf_op jit(solution)/shard_map/ppermute | solution.py:27
  54.3 8.9 %collective-permute-start.10 = (bf16[128,1024]{1,0:T(8,128)(2,1)S(1)}, bf16[128,1024]{1,0:T(8,128)(2,1)S(1)}, u32[]{:S(2)}, u32[]{:S(2)}) collective-permute-start(bf16[128,1024]{1,0:T(8,128)(2,1)S(1)} %fusion.138), channel_id=1, source_target_pairs={{1,0},{2,1},{3,2},{4,3},{5,4},{6,5},{7,6},{9,8},{10,9},{11,10},{12... | collective-permute-start | bytes 786440 | tf_op jit(solution)/shard_map/ppermute | solution.py:27
  59.9 8.3 %collective-permute-start.11 = (bf16[128,1024]{1,0:T(8,128)(2,1)S(1)}, bf16[128,1024]{1,0:T(8,128)(2,1)S(1)}, u32[]{:S(2)}, u32[]{:S(2)}) collective-permute-start(bf16[128,1024]{1,0:T(8,128)(2,1)S(1)} %broadcast_select_fusion.3), channel_id=1, source_target_pairs={{1,0},{2,1},{3,2},{4,3},{5,4},{6,5},{7,6},{9,8},{10,9},{11,10},{12... | collective-permute-start | bytes 786440 | tf_op jit(solution)/shard_map/ppermute | solution.py:27
  69.3 7.4 %collective-permute-start.12 = (bf16[128,1024]{1,0:T(8,128)(2,1)S(1)}, bf16[128,1024]{1,0:T(8,128)(2,1)S(1)}, u32[]{:S(2)}, u32[]{:S(2)}) collective-permute-start(bf16[128,1024]{1,0:T(8,128)(2,1)S(1)} %fusion.135), channel_id=1, source_target_pairs={{8,0},{9,1},{10,2},{11,3},{12,4},{13,5},{14,6},{15,7},{16,8},{17,9... | collective-permute-start | bytes 786440 | tf_op jit(solution)/shard_map/ppermute | solution.py:27
  71.1 5.8 %collective-permute-start.13 = (bf16[128,1024]{1,0:T(8,128)(2,1)S(1)}, bf16[128,1024]{1,0:T(8,128)(2,1)S(1)}, u32[]{:S(2)}, u32[]{:S(2)}) collective-permute-start(bf16[128,1024]{1,0:T(8,128)(2,1)S(1)} %fusion.135), channel_id=1, source_target_pairs={{1,0},{2,1},{3,2},{4,3},{5,4},{6,5},{7,6},{9,8},{10,9},{11,10},{12... | collective-permute-start | bytes 786440 | tf_op jit(solution)/shard_map/ppermute | solution.py:27
  76.8 5.8 %collective-permute-start.14 = (bf16[128,1024]{1,0:T(8,128)(2,1)S(1)}, bf16[128,1024]{1,0:T(8,128)(2,1)S(1)}, u32[]{:S(2)}, u32[]{:S(2)}) collective-permute-start(bf16[128,1024]{1,0:T(8,128)(2,1)S(1)} %broadcast_select_fusion.4), channel_id=1, source_target_pairs={{1,0},{2,1},{3,2},{4,3},{5,4},{6,5},{7,6},{9,8},{10,9},{11,10},{12... | collective-permute-start | bytes 786440 | tf_op jit(solution)/shard_map/ppermute | solution.py:27
  83.7 9.7 %collective-permute-start.15 = (bf16[128,1024]{1,0:T(8,128)(2,1)S(1)}, bf16[128,1024]{1,0:T(8,128)(2,1)S(1)}, u32[]{:S(2)}, u32[]{:S(2)}) collective-permute-start(bf16[128,1024]{1,0:T(8,128)(2,1)S(1)} %fusion.132), channel_id=1, source_target_pairs={{8,0},{9,1},{10,2},{11,3},{12,4},{13,5},{14,6},{15,7},{16,8},{17,9... | collective-permute-start | bytes 786440 | tf_op jit(solution)/shard_map/ppermute | solution.py:27
  87.3 6.7 %collective-permute-start.16 = (bf16[128,1024]{1,0:T(8,128)(2,1)S(1)}, bf16[128,1024]{1,0:T(8,128)(2,1)S(1)}, u32[]{:S(2)}, u32[]{:S(2)}) collective-permute-start(bf16[128,1024]{1,0:T(8,128)(2,1)S(1)} %fusion.132), channel_id=1, source_target_pairs={{1,0},{2,1},{3,2},{4,3},{5,4},{6,5},{7,6},{9,8},{10,9},{11,10},{12... | collective-permute-start | bytes 786440 | tf_op jit(solution)/shard_map/ppermute | solution.py:27
  93.5 5.8 %collective-permute-start.17 = (bf16[128,1024]{1,0:T(8,128)(2,1)S(1)}, bf16[128,1024]{1,0:T(8,128)(2,1)S(1)}, u32[]{:S(2)}, u32[]{:S(2)}) collective-permute-start(bf16[128,1024]{1,0:T(8,128)(2,1)S(1)} %broadcast_select_fusion.5), channel_id=1, source_target_pairs={{1,0},{2,1},{3,2},{4,3},{5,4},{6,5},{7,6},{9,8},{10,9},{11,10},{12... | collective-permute-start | bytes 786440 | tf_op jit(solution)/shard_map/ppermute | solution.py:27
  100.4 10.0 %collective-permute-start.18 = (bf16[128,1024]{1,0:T(8,128)(2,1)S(1)}, bf16[128,1024]{1,0:T(8,128)(2,1)S(1)}, u32[]{:S(2)}, u32[]{:S(2)}) collective-permute-start(bf16[128,1024]{1,0:T(8,128)(2,1)S(1)} %fusion.129), channel_id=1, source_target_pairs={{8,0},{9,1},{10,2},{11,3},{12,4},{13,5},{14,6},{15,7},{16,8},{17,9... | collective-permute-start | bytes 786440 | tf_op jit(solution)/shard_map/ppermute | solution.py:27
  104.4 6.3 %collective-permute-start.19 = (bf16[128,1024]{1,0:T(8,128)(2,1)S(1)}, bf16[128,1024]{1,0:T(8,128)(2,1)S(1)}, u32[]{:S(2)}, u32[]{:S(2)}) collective-permute-start(bf16[128,1024]{1,0:T(8,128)(2,1)S(1)} %fusion.129), channel_id=1, source_target_pairs={{1,0},{2,1},{3,2},{4,3},{5,4},{6,5},{7,6},{9,8},{10,9},{11,10},{12... | collective-permute-start | bytes 786440 | tf_op jit(solution)/shard_map/ppermute | solution.py:27
  110.5 5.8 %collective-permute-start.20 = (bf16[128,1024]{1,0:T(8,128)(2,1)S(1)}, bf16[128,1024]{1,0:T(8,128)(2,1)S(1)}, u32[]{:S(2)}, u32[]{:S(2)}) collective-permute-start(bf16[128,1024]{1,0:T(8,128)(2,1)S(1)} %broadcast_select_fusion.6), channel_id=1, source_target_pairs={{1,0},{2,1},{3,2},{4,3},{5,4},{6,5},{7,6},{9,8},{10,9},{11,10},{12... | collective-permute-start | bytes 786440 | tf_op jit(solution)/shard_map/ppermute | solution.py:27

commit v2 on v1

v2 whole, which is shorter than its diff:
```python
import functools

import jax
import jax.numpy as jnp
from jax import lax
from jax.experimental import pallas as pl
from jax.experimental.pallas import tpu as pltpu
from jax.sharding import PartitionSpec as P

TICKS = 8
AXES = ("row", "col")


def closed(route, rows, cols):
    every = [(r, c) for r in range(rows) for c in range(cols)]
    sources, targets = {a for a, _ in route}, {b for _, b in route}
    free = [p for p in every if p not in targets]
    for a in [p for p in every if p not in sources]:
        far = lambda b: (b == a, abs(b[0] - a[0]) + abs(b[1] // 2 - a[1] // 2), b[1] != a[1])
        b = min(free, key=far)
        free.remove(b)
        route = route + [(a, b)]
    return [(a[0] * cols + a[1], b[0] * cols + b[1]) for a, b in route if a != b]


def shift(block, dr, dc):
    rows, cols = lax.axis_size("row"), lax.axis_size("col")
    inside = lambda r, c: 0 <= r < rows and 0 <= c < cols
    every = [(r, c) for r in range(rows) for c in range(cols)]
    route = [((r, c), (r + dr, c + dc)) for r, c in every if inside(r + dr, c + dc)]
    return lax.ppermute(block, AXES, closed(route, rows, cols))


TILE = 16
SPARE = (1, 3)


def capacities(batches):
    part = lambda tick, spare: min(batches, -(-batches * tick // (TICKS * TILE)) * TILE + spare * TILE)
    levels = [tuple(part(tick, spare) for tick in range(1, TICKS)) for spare in SPARE]
    return levels + [(batches,) * (TICKS - 1)]


def resident(x):
    def kernel(x_ref, o_ref, sem):
        copy = pltpu.make_async_copy(x_ref, o_ref, sem)
        copy.start()
        copy.wait()

    return pl.pallas_call(
        kernel,
        out_shape=pltpu.VMEM(x.shape, x.dtype),
        in_specs=[pl.BlockSpec(memory_space=pl.ANY)],
        out_specs=pl.BlockSpec(memory_space=pltpu.VMEM),
        scratch_shapes=[pltpu.SemaphoreType.DMA],
        compiler_params=pltpu.CompilerParams(vmem_limit_bytes=1 << 20),
    )(x)


def exchange(block, s, form):
    up = shift(block, s, 0)
    if form == "G":
        corner = shift(block, s, s)
    left = shift(block, 0, s)
    if form == "D":
        corner = None
    return up, left, corner


def sweep(sizes):
    def run(traces, source, operators, start_tick, *seen):
        for tick in range(1, TICKS):
            s = 1 if tick < TICKS // 2 else -1
            has_row, has_col, has_both = seen[:3] if s > 0 else seen[3:]
            n = sizes[tick - 1]
            form = "G" if n <= 72 else "D"
            keep = lambda x, first: jnp.where((first[:n] < tick)[:, None], x, jnp.zeros_like(x))
            up, left, corner = exchange(traces[:n], s, form)
            if tick == 1:
                ops = resident(operators)
            up, left = keep(up, has_row), keep(left, has_col)
            if corner is None:
                corner = keep(shift(up, 0, s), has_col)
            else:
                corner = keep(corner, has_both)
            summed = source[:n]
            for mat, block in enumerate((up, left, corner)):
                summed = summed + jnp.dot(block, ops[mat], preferred_element_type=jnp.float32)
            if n < source.shape[0]:
                summed = jnp.concatenate([summed, source[n:]], axis=0)
            running = (tick >= start_tick)[:, None]
            traces = jnp.where(running, summed, 0.0).astype(jnp.bfloat16)
        return traces

    return run


def body(rhs, operators, positions, start_tick):
    rows, cols = lax.axis_size("row"), lax.axis_size("col")
    batches, width = rhs.shape[2:]
    i, j = lax.axis_index("row"), lax.axis_index("col")

    number = jnp.arange(batches, dtype=jnp.int32)
    key = start_tick * batches + number
    rank = jnp.sum((key[None, :] < key[:, None]).astype(jnp.int32), axis=1)
    chosen = rank[None, :] == number[:, None]
    place = chosen.astype(jnp.bfloat16)
    levels = capacities(batches)
    lost = [
        functools.reduce(jnp.logical_or, [(rank >= n) & (start_tick < tick) for tick, n in enumerate(sizes, 1)])
        for sizes in levels[:-1]
    ]
    level = jnp.max(sum(one.astype(jnp.int32) for one in lost))
    sort = lambda v: jnp.sum(jnp.where(chosen, v[None, :], 0), axis=1)
    start_tick, positions = sort(start_tick), sort(positions)

    local_point = positions - (i * cols + j) * width
    column_ids = lax.broadcasted_iota(jnp.int32, (batches, width), 1)
    spike = (local_point[:, None] == column_ids).astype(jnp.float32)
    source = jnp.dot(place, rhs[0, 0], preferred_element_type=jnp.float32) + 4.0 * spike
    traces = jnp.where((0 >= start_tick)[:, None], source, 0.0).astype(jnp.bfloat16)
    seen = {}
    for s in (1, -1):
        row_ok, col_ok = (i - s >= 0) & (i - s < rows), (j - s >= 0) & (j - s < cols)
        seen[s] = tuple(jnp.where(ok, start_tick, TICKS) for ok in (row_ok, col_ok, row_ok & col_ok))
    traces = lax.switch(
        level, [sweep(sizes) for sizes in levels], traces, source, operators[0, 0], start_tick, *seen[1], *seen[-1]
    )
    back = lax.dot_general(place, traces, (((0,), (0,)), ((), ())), preferred_element_type=jnp.float32)
    return back.astype(jnp.bfloat16)[None, None]


def solution(mesh):
    placed = (P("row", "col", None, None), P("row", "col", None, None, None), P(), P())
    return jax.shard_map(
        body, mesh=mesh, in_specs=placed, out_specs=P("row", "col", None, None), check_vma=False
    )
```

time: 118 us -> 94.5 us (0.80)
  the two profiles are of different devices: /device:TPU:1 before, /device:TPU:0 now
where the time goes in v2:
time: 94.5 us; the launch traced here: 94.3 us
  starting transfers between devices  40 us (42%)
  waiting for transfers between devices  34.1 us (36%)
  matrix products  12 us (13%)
  other arithmetic  4 us (4%)
  Pallas kernels  2.8 us (3%)
    ppermute x21, starting transfers between devices, shift(): return lax.ppermute(block, AXES, closed(route, rows, cols))  40 us
    ppermute x21, waiting for transfers between devices, shift(): return lax.ppermute(block, AXES, closed(route, rows, cols))  34.1 us
    dot_general x21, matrix products, run(): jnp.dot(block, ops[mat], preferred_element_type=jnp.float32)  10.8 us
    pallas_call x1, Pallas kernels, resident(): pl.pallas_call(kernel, out_shape=pltpu.VMEM(x.shape, x.dtype), in_specs=[...  2.8 us
  transfers between devices with their start and end apart: 21, of which 14 were waited for; matrix products, arithmetic and copies ran while one was open for 6% of the time, Pallas kernels for 3%

profile of v2, /device:TPU:0, one launch (start us, length us, event | category | flops | bytes accessed | tf_op | source)
XLA Modules:
  0.0 94.3 jit_solution(420327822549182111)
XLA Ops:
  0.9 0.8 select_reduce_fusion
  2.0 1.3 %add_reduce_fusion = s32[]{:T(128)} fusion(s32[128]{0:T(128)} %param.10, s32[128]{0:T(128)S(1)} %convert_reduce_fusion), kind=kLoop, calls=%fused_computation.451 | loop fusion | flops 5503 | bytes 1028 | tf_op jit(solution)/shard_map/reduce_max | solution.py:113
  3.9 89.4 %conditional.3 = (bf16[128,1024]{1,0:T(8,128)(2,1)S(1)}) conditional(s32[]{:T(128)} %clamp.3, (s32[128]{0:T(128)S(1)}, s32[128]{0:T(128)S(1)}, f32[128,1024]{1,0:T(8,128)S(1)}, s32[128]{0:T(128)S(1)}, bf16[128,1024]{1,0:T(8,128)(2,1)S(1)}, /*index=5*/bf16[3,1024,1024]{2,1,0:T(8,128)(2,1)}, s32[128]{0:T(128)S(1)}, pred[]{:T(512)}, ...), branch_computations={%region_4.5_spmd, %region_5.6_spmd, %region_6.7_spmd} | conditional | flops 5644356096 | bytes 139151360
  4.5 3.8 %collective-permute-start.2 = (bf16[32,1024]{1,0:T(8,128)(2,1)S(1)}, bf16[32,1024]{1,0:T(8,128)(2,1)S(1)}, u32[]{:S(2)}, u32[]{:S(2)}) collective-permute-start(bf16[32,1024]{1,0:T(8,128)(2,1)S(1)} %slice.132), channel_id=1, source_target_pairs={{0,9},{1,10},{2,11},{3,12},{4,13},{5,14},{6,15},{8,17},{9,18},{10,... | collective-permute-start | bytes 196616 | tf_op jit(solution)/shard_map/cond/branch_0_fun/ppermute | solution.py:31
  8.3 1.6 %collective-permute-start = (bf16[32,1024]{1,0:T(8,128)(2,1)S(1)}, bf16[32,1024]{1,0:T(8,128)(2,1)S(1)}, u32[]{:S(2)}, u32[]{:S(2)}) collective-permute-start(bf16[32,1024]{1,0:T(8,128)(2,1)S(1)} %slice.132), channel_id=1, source_target_pairs={{0,8},{1,9},{2,10},{3,11},{4,12},{5,13},{6,14},{7,15},{8,16},{9,17... | collective-permute-start | bytes 196616 | tf_op jit(solution)/shard_map/cond/branch_0_fun/ppermute | solution.py:31
  10.0 2.8 %branch_0_fun.1 = bf16[3,1024,1024]{2,1,0:T(8,128)(2,1)S(1)} custom-call(bf16[3,1024,1024]{2,1,0:T(8,128)(2,1)} %get-tuple-element.87.x_ref), custom_call_target="tpu_custom_call" | custom-call | tf_op jit(solution)/shard_map/cond/branch_0_fun/pallas_call | solution.py:50
  15.1 2.3 %collective-permute-start.5 = (bf16[48,1024]{1,0:T(8,128)(2,1)S(1)}, bf16[48,1024]{1,0:T(8,128)(2,1)S(1)}, u32[]{:S(2)}, u32[]{:S(2)}) collective-permute-start(bf16[48,1024]{1,0:T(8,128)(2,1)S(1)} %fusion.47), channel_id=1, source_target_pairs={{0,9},{1,10},{2,11},{3,12},{4,13},{5,14},{6,15},{8,17},{9,18},{10,... | collective-permute-start | bytes 294920 | tf_op jit(solution)/shard_map/cond/branch_0_fun/ppermute | solution.py:31
  17.7 2.2 %collective-permute-done.4 = bf16[48,1024]{1,0:T(8,128)(2,1)S(1)} collective-permute-done((bf16[48,1024]{1,0:T(8,128)(2,1)S(1)}, bf16[48,1024]{1,0:T(8,128)(2,1)S(1)}, u32[]{:S(2)}, u32[]{:S(2)}) %collective-permute-start.4) | collective-permute-done | bytes 98336 | tf_op jit(solution)/shard_map/cond/branch_0_fun/ppermute | solution.py:31
  20.5 3.4 %collective-permute-done.5 = bf16[48,1024]{1,0:T(8,128)(2,1)S(1)} collective-permute-done((bf16[48,1024]{1,0:T(8,128)(2,1)S(1)}, bf16[48,1024]{1,0:T(8,128)(2,1)S(1)}, u32[]{:S(2)}, u32[]{:S(2)}) %collective-permute-start.5) | collective-permute-done | bytes 98336 | tf_op jit(solution)/shard_map/cond/branch_0_fun/ppermute | solution.py:31
  25.0 1.1 %collective-permute-start.7 = (bf16[64,1024]{1,0:T(8,128)(2,1)S(1)}, bf16[64,1024]{1,0:T(8,128)(2,1)S(1)}, u32[]{:S(2)}, u32[]{:S(2)}) collective-permute-start(bf16[64,1024]{1,0:T(8,128)(2,1)S(1)} %fusion.37), channel_id=1, source_target_pairs={{0,1},{1,2},{2,3},{3,4},{4,5},{5,6},{6,7},{8,9},{9,10},{10,11},{11... | collective-permute-start | bytes 393224 | tf_op jit(solution)/shard_map/cond/branch_0_fun/ppermute | solution.py:31
  26.8 3.5 %collective-permute-done.7 = bf16[64,1024]{1,0:T(8,128)(2,1)S(1)} collective-permute-done((bf16[64,1024]{1,0:T(8,128)(2,1)S(1)}, bf16[64,1024]{1,0:T(8,128)(2,1)S(1)}, u32[]{:S(2)}, u32[]{:S(2)}) %collective-permute-start.7) | collective-permute-done | bytes 131104 | tf_op jit(solution)/shard_map/cond/branch_0_fun/ppermute | solution.py:31
  30.9 5.2 %collective-permute-done.8 = bf16[64,1024]{1,0:T(8,128)(2,1)S(1)} collective-permute-done((bf16[64,1024]{1,0:T(8,128)(2,1)S(1)}, bf16[64,1024]{1,0:T(8,128)(2,1)S(1)}, u32[]{:S(2)}, u32[]{:S(2)}) %collective-permute-start.8) | collective-permute-done | bytes 131104 | tf_op jit(solution)/shard_map/cond/branch_0_fun/ppermute | solution.py:31
  37.3 2.6 %collective-permute-start.10 = (bf16[80,1024]{1,0:T(8,128)(2,1)S(1)}, bf16[80,1024]{1,0:T(8,128)(2,1)S(1)}, u32[]{:S(2)}, u32[]{:S(2)}) collective-permute-start(bf16[80,1024]{1,0:T(8,128)(2,1)S(1)} %fusion.35), channel_id=1, source_target_pairs={{1,0},{2,1},{3,2},{4,3},{5,4},{6,5},{7,6},{9,8},{10,9},{11,10},{12... | collective-permute-start | bytes 491528 | tf_op jit(solution)/shard_map/cond/branch_0_fun/ppermute | solution.py:31
  39.9 3.6 %collective-permute-done.9 = bf16[80,1024]{1,0:T(8,128)(2,1)S(1)} collective-permute-done((bf16[80,1024]{1,0:T(8,128)(2,1)S(1)}, bf16[80,1024]{1,0:T(8,128)(2,1)S(1)}, u32[]{:S(2)}, u32[]{:S(2)}) %collective-permute-start.9) | collective-permute-done | bytes 163872 | tf_op jit(solution)/shard_map/cond/branch_0_fun/ppermute | solution.py:31
  43.6 1.6 %collective-permute-start.11 = (bf16[80,1024]{1,0:T(8,128)(2,1)S(1)}, bf16[80,1024]{1,0:T(8,128)(2,1)S(1)}, u32[]{:S(2)}, u32[]{:S(2)}) collective-permute-start(bf16[80,1024]{1,0:T(8,128)(2,1)S(1)} %broadcast_select_fusion.3), channel_id=1, source_target_pairs={{1,0},{2,1},{3,2},{4,3},{5,4},{6,5},{7,6},{9,8},{10,9},{11,10},{12... | collective-permute-start | bytes 491528 | tf_op jit(solution)/shard_map/cond/branch_0_fun/ppermute | solution.py:31
  45.8 2.3 %collective-permute-done.11 = bf16[80,1024]{1,0:T(8,128)(2,1)S(1)} collective-permute-done((bf16[80,1024]{1,0:T(8,128)(2,1)S(1)}, bf16[80,1024]{1,0:T(8,128)(2,1)S(1)}, u32[]{:S(2)}, u32[]{:S(2)}) %collective-permute-start.11) | collective-permute-done | bytes 163872 | tf_op jit(solution)/shard_map/cond/branch_0_fun/ppermute | solution.py:31
  49.2 2.4 %collective-permute-start.12 = (bf16[96,1024]{1,0:T(8,128)(2,1)S(1)}, bf16[96,1024]{1,0:T(8,128)(2,1)S(1)}, u32[]{:S(2)}, u32[]{:S(2)}) collective-permute-start(bf16[96,1024]{1,0:T(8,128)(2,1)S(1)} %fusion.33), channel_id=1, source_target_pairs={{8,0},{9,1},{10,2},{11,3},{12,4},{13,5},{14,6},{15,7},{16,8},{17,9... | collective-permute-start | bytes 589832 | tf_op jit(solution)/shard_map/cond/branch_0_fun/ppermute | solution.py:31
  51.6 2.5 %collective-permute-start.13 = (bf16[96,1024]{1,0:T(8,128)(2,1)S(1)}, bf16[96,1024]{1,0:T(8,128)(2,1)S(1)}, u32[]{:S(2)}, u32[]{:S(2)}) collective-permute-start(bf16[96,1024]{1,0:T(8,128)(2,1)S(1)} %fusion.33), channel_id=1, source_target_pairs={{1,0},{2,1},{3,2},{4,3},{5,4},{6,5},{7,6},{9,8},{10,9},{11,10},{12... | collective-permute-start | bytes 589832 | tf_op jit(solution)/shard_map/cond/branch_0_fun/ppermute | solution.py:31
  54.2 1.5 %collective-permute-done.12 = bf16[96,1024]{1,0:T(8,128)(2,1)S(1)} collective-permute-done((bf16[96,1024]{1,0:T(8,128)(2,1)S(1)}, bf16[96,1024]{1,0:T(8,128)(2,1)S(1)}, u32[]{:S(2)}, u32[]{:S(2)}) %collective-permute-start.12) | collective-permute-done | bytes 196640 | tf_op jit(solution)/shard_map/cond/branch_0_fun/ppermute | solution.py:31
  55.7 2.1 %collective-permute-start.14 = (bf16[96,1024]{1,0:T(8,128)(2,1)S(1)}, bf16[96,1024]{1,0:T(8,128)(2,1)S(1)}, u32[]{:S(2)}, u32[]{:S(2)}) collective-permute-start(bf16[96,1024]{1,0:T(8,128)(2,1)S(1)} %broadcast_select_fusion.2), channel_id=1, source_target_pairs={{1,0},{2,1},{3,2},{4,3},{5,4},{6,5},{7,6},{9,8},{10,9},{11,10},{12... | collective-permute-start | bytes 589832 | tf_op jit(solution)/shard_map/cond/branch_0_fun/ppermute | solution.py:31
  58.4 2.7 %collective-permute-done.14 = bf16[96,1024]{1,0:T(8,128)(2,1)S(1)} collective-permute-done((bf16[96,1024]{1,0:T(8,128)(2,1)S(1)}, bf16[96,1024]{1,0:T(8,128)(2,1)S(1)}, u32[]{:S(2)}, u32[]{:S(2)}) %collective-permute-start.14) | collective-permute-done | bytes 196640 | tf_op jit(solution)/shard_map/cond/branch_0_fun/ppermute | solution.py:31
  62.2 3.9 %collective-permute-start.15 = (bf16[112,1024]{1,0:T(8,128)(2,1)S(1)}, bf16[112,1024]{1,0:T(8,128)(2,1)S(1)}, u32[]{:S(2)}, u32[]{:S(2)}) collective-permute-start(bf16[112,1024]{1,0:T(8,128)(2,1)S(1)} %fusion.31), channel_id=1, source_target_pairs={{8,0},{9,1},{10,2},{11,3},{12,4},{13,5},{14,6},{15,7},{16,8},{17,9... | collective-permute-start | bytes 688136 | tf_op jit(solution)/shard_map/cond/branch_0_fun/ppermute | solution.py:31
  66.2 2.6 %collective-permute-start.16 = (bf16[112,1024]{1,0:T(8,128)(2,1)S(1)}, bf16[112,1024]{1,0:T(8,128)(2,1)S(1)}, u32[]{:S(2)}, u32[]{:S(2)}) collective-permute-start(bf16[112,1024]{1,0:T(8,128)(2,1)S(1)} %fusion.31), channel_id=1, source_target_pairs={{1,0},{2,1},{3,2},{4,3},{5,4},{6,5},{7,6},{9,8},{10,9},{11,10},{12... | collective-permute-start | bytes 688136 | tf_op jit(solution)/shard_map/cond/branch_0_fun/ppermute | solution.py:31
  68.8 1.2 %collective-permute-done.15 = bf16[112,1024]{1,0:T(8,128)(2,1)S(1)} collective-permute-done((bf16[112,1024]{1,0:T(8,128)(2,1)S(1)}, bf16[112,1024]{1,0:T(8,128)(2,1)S(1)}, u32[]{:S(2)}, u32[]{:S(2)}) %collective-permute-start.15) | collective-permute-done | bytes 229408 | tf_op jit(solution)/shard_map/cond/branch_0_fun/ppermute | solution.py:31
  70.0 1.7 %collective-permute-start.17 = (bf16[112,1024]{1,0:T(8,128)(2,1)S(1)}, bf16[112,1024]{1,0:T(8,128)(2,1)S(1)}, u32[]{:S(2)}, u32[]{:S(2)}) collective-permute-start(bf16[112,1024]{1,0:T(8,128)(2,1)S(1)} %broadcast_select_fusion.1), channel_id=1, source_target_pairs={{1,0},{2,1},{3,2},{4,3},{5,4},{6,5},{7,6},{9,8},{10,9},{11,10},{12... | collective-permute-start | bytes 688136 | tf_op jit(solution)/shard_map/cond/branch_0_fun/ppermute | solution.py:31
  72.8 2.5 %collective-permute-done.17 = bf16[112,1024]{1,0:T(8,128)(2,1)S(1)} collective-permute-done((bf16[112,1024]{1,0:T(8,128)(2,1)S(1)}, bf16[112,1024]{1,0:T(8,128)(2,1)S(1)}, u32[]{:S(2)}, u32[]{:S(2)}) %collective-permute-start.17) | collective-permute-done | bytes 229408 | tf_op jit(solution)/shard_map/cond/branch_0_fun/ppermute | solution.py:31
  76.5 4.0 %collective-permute-start.18 = (bf16[128,1024]{1,0:T(8,128)(2,1)S(1)}, bf16[128,1024]{1,0:T(8,128)(2,1)S(1)}, u32[]{:S(2)}, u32[]{:S(2)}) collective-permute-start(bf16[128,1024]{1,0:T(8,128)(2,1)S(1)} %fusion.29), channel_id=1, source_target_pairs={{8,0},{9,1},{10,2},{11,3},{12,4},{13,5},{14,6},{15,7},{16,8},{17,9... | collective-permute-start | bytes 786440 | tf_op jit(solution)/shard_map/cond/branch_0_fun/ppermute | solution.py:31
  80.5 2.5 %collective-permute-start.19 = (bf16[128,1024]{1,0:T(8,128)(2,1)S(1)}, bf16[128,1024]{1,0:T(8,128)(2,1)S(1)}, u32[]{:S(2)}, u32[]{:S(2)}) collective-permute-start(bf16[128,1024]{1,0:T(8,128)(2,1)S(1)} %fusion.29), channel_id=1, source_target_pairs={{1,0},{2,1},{3,2},{4,3},{5,4},{6,5},{7,6},{9,8},{10,9},{11,10},{12... | collective-permute-start | bytes 786440 | tf_op jit(solution)/shard_map/cond/branch_0_fun/ppermute | solution.py:31
  83.0 1.6 %collective-permute-done.18 = bf16[128,1024]{1,0:T(8,128)(2,1)S(1)} collective-permute-done((bf16[128,1024]{1,0:T(8,128)(2,1)S(1)}, bf16[128,1024]{1,0:T(8,128)(2,1)S(1)}, u32[]{:S(2)}, u32[]{:S(2)}) %collective-permute-start.18) | collective-permute-done | bytes 262176 | tf_op jit(solution)/shard_map/cond/branch_0_fun/ppermute | solution.py:31
  84.8 3.4 %collective-permute-start.20 = (bf16[128,1024]{1,0:T(8,128)(2,1)S(1)}, bf16[128,1024]{1,0:T(8,128)(2,1)S(1)}, u32[]{:S(2)}, u32[]{:S(2)}) collective-permute-start(bf16[128,1024]{1,0:T(8,128)(2,1)S(1)} %broadcast_select_fusion), channel_id=1, source_target_pairs={{1,0},{2,1},{3,2},{4,3},{5,4},{6,5},{7,6},{9,8},{10,9},{11,10},{12... | collective-permute-start | bytes 786440 | tf_op jit(solution)/shard_map/cond/branch_0_fun/ppermute | solution.py:31
  88.7 3.4 %collective-permute-done.20 = bf16[128,1024]{1,0:T(8,128)(2,1)S(1)} collective-permute-done((bf16[128,1024]{1,0:T(8,128)(2,1)S(1)}, bf16[128,1024]{1,0:T(8,128)(2,1)S(1)}, u32[]{:S(2)}, u32[]{:S(2)}) %collective-permute-start.20) | collective-permute-done | bytes 262176 | tf_op jit(solution)/shard_map/cond/branch_0_fun/ppermute | solution.py:31
  93.3 1.0 %fusion.305 = bf16[1,1,128,1024]{3,2,1,0:T(8,128)(2,1)} fusion(bf16[128,1024]{1,0:T(8,128)(2,1)S(1)} %get-tuple-element.177, s32[128]{0:T(128)S(1)} %convert_reduce_fusion), kind=kOutput, calls=%fused_computation.433 | convolution fusion | flops 33701888 | bytes 524800 | tf_op jit(solution)/shard_map/dot_general | solution.py:129
  (79 shorter events, 15.8 us)
Async XLA Ops:
  0.0 1.7 %copy-start = (bf16[1,1,128,1024]{3,2,1,0:T(8,128)(2,1)S(1)}, bf16[1,1,128,1024]{3,2,1,0:T(8,128)(2,1)}, u32[]{:S(2)}) copy-start(bf16[1,1,128,1024]{3,2,1,0:T(8,128)(2,1)} %param.7) | copy-start | bytes 786436
  4.0 8.8 %collective-permute-start.1 = (bf16[32,1024]{1,0:T(8,128)(2,1)S(1)}, bf16[32,1024]{1,0:T(8,128)(2,1)S(1)}, u32[]{:S(2)}, u32[]{:S(2)}) collective-permute-start(bf16[32,1024]{1,0:T(8,128)(2,1)S(1)} %slice.132), channel_id=1, source_target_pairs={{0,1},{1,2},{2,3},{3,4},{4,5},{5,6},{6,7},{8,9},{9,10},{10,11},{11... | collective-permute-start | bytes 196616 | tf_op jit(solution)/shard_map/cond/branch_0_fun/ppermute | solution.py:31
  4.5 8.8 %collective-permute-start.2 = (bf16[32,1024]{1,0:T(8,128)(2,1)S(1)}, bf16[32,1024]{1,0:T(8,128)(2,1)S(1)}, u32[]{:S(2)}, u32[]{:S(2)}) collective-permute-start(bf16[32,1024]{1,0:T(8,128)(2,1)S(1)} %slice.132), channel_id=1, source_target_pairs={{0,9},{1,10},{2,11},{3,12},{4,13},{5,14},{6,15},{8,17},{9,18},{10,... | collective-permute-start | bytes 196616 | tf_op jit(solution)/shard_map/cond/branch_0_fun/ppermute | solution.py:31
  8.3 6.1 %collective-permute-start = (bf16[32,1024]{1,0:T(8,128)(2,1)S(1)}, bf16[32,1024]{1,0:T(8,128)(2,1)S(1)}, u32[]{:S(2)}, u32[]{:S(2)}) collective-permute-start(bf16[32,1024]{1,0:T(8,128)(2,1)S(1)} %slice.132), channel_id=1, source_target_pairs={{0,8},{1,9},{2,10},{3,11},{4,12},{5,13},{6,14},{7,15},{8,16},{9,17... | collective-permute-start | bytes 196616 | tf_op jit(solution)/shard_map/cond/branch_0_fun/ppermute | solution.py:31
  15.0 5.0 %collective-permute-start.4 = (bf16[48,1024]{1,0:T(8,128)(2,1)S(1)}, bf16[48,1024]{1,0:T(8,128)(2,1)S(1)}, u32[]{:S(2)}, u32[]{:S(2)}) collective-permute-start(bf16[48,1024]{1,0:T(8,128)(2,1)S(1)} %fusion.47), channel_id=1, source_target_pairs={{0,1},{1,2},{2,3},{3,4},{4,5},{5,6},{6,7},{8,9},{9,10},{10,11},{11... | collective-permute-start | bytes 294920 | tf_op jit(solution)/shard_map/cond/branch_0_fun/ppermute | solution.py:31
  15.1 8.7 %collective-permute-start.5 = (bf16[48,1024]{1,0:T(8,128)(2,1)S(1)}, bf16[48,1024]{1,0:T(8,128)(2,1)S(1)}, u32[]{:S(2)}, u32[]{:S(2)}) collective-permute-start(bf16[48,1024]{1,0:T(8,128)(2,1)S(1)} %fusion.47), channel_id=1, source_target_pairs={{0,9},{1,10},{2,11},{3,12},{4,13},{5,14},{6,15},{8,17},{9,18},{10,... | collective-permute-start | bytes 294920 | tf_op jit(solution)/shard_map/cond/branch_0_fun/ppermute | solution.py:31
  17.4 6.9 %collective-permute-start.3 = (bf16[48,1024]{1,0:T(8,128)(2,1)S(1)}, bf16[48,1024]{1,0:T(8,128)(2,1)S(1)}, u32[]{:S(2)}, u32[]{:S(2)}) collective-permute-start(bf16[48,1024]{1,0:T(8,128)(2,1)S(1)} %fusion.47), channel_id=1, source_target_pairs={{0,8},{1,9},{2,10},{3,11},{4,12},{5,13},{6,14},{7,15},{8,16},{9,17... | collective-permute-start | bytes 294920 | tf_op jit(solution)/shard_map/cond/branch_0_fun/ppermute | solution.py:31
  25.0 5.3 %collective-permute-start.7 = (bf16[64,1024]{1,0:T(8,128)(2,1)S(1)}, bf16[64,1024]{1,0:T(8,128)(2,1)S(1)}, u32[]{:S(2)}, u32[]{:S(2)}) collective-permute-start(bf16[64,1024]{1,0:T(8,128)(2,1)S(1)} %fusion.37), channel_id=1, source_target_pairs={{0,1},{1,2},{2,3},{3,4},{4,5},{5,6},{6,7},{8,9},{9,10},{10,11},{11... | collective-permute-start | bytes 393224 | tf_op jit(solution)/shard_map/cond/branch_0_fun/ppermute | solution.py:31
  26.1 10.0 %collective-permute-start.8 = (bf16[64,1024]{1,0:T(8,128)(2,1)S(1)}, bf16[64,1024]{1,0:T(8,128)(2,1)S(1)}, u32[]{:S(2)}, u32[]{:S(2)}) collective-permute-start(bf16[64,1024]{1,0:T(8,128)(2,1)S(1)} %fusion.37), channel_id=1, source_target_pairs={{0,9},{1,10},{2,11},{3,12},{4,13},{5,14},{6,15},{8,17},{9,18},{10,... | collective-permute-start | bytes 393224 | tf_op jit(solution)/shard_map/cond/branch_0_fun/ppermute | solution.py:31
  26.3 10.3 %collective-permute-start.6 = (bf16[64,1024]{1,0:T(8,128)(2,1)S(1)}, bf16[64,1024]{1,0:T(8,128)(2,1)S(1)}, u32[]{:S(2)}, u32[]{:S(2)}) collective-permute-start(bf16[64,1024]{1,0:T(8,128)(2,1)S(1)} %fusion.37), channel_id=1, source_target_pairs={{0,8},{1,9},{2,10},{3,11},{4,12},{5,13},{6,14},{7,15},{8,16},{9,17... | collective-permute-start | bytes 393224 | tf_op jit(solution)/shard_map/cond/branch_0_fun/ppermute | solution.py:31
  37.3 6.2 %collective-permute-start.9 = (bf16[80,1024]{1,0:T(8,128)(2,1)S(1)}, bf16[80,1024]{1,0:T(8,128)(2,1)S(1)}, u32[]{:S(2)}, u32[]{:S(2)}) collective-permute-start(bf16[80,1024]{1,0:T(8,128)(2,1)S(1)} %fusion.35), channel_id=1, source_target_pairs={{8,0},{9,1},{10,2},{11,3},{12,4},{13,5},{14,6},{15,7},{16,8},{17,9... | collective-permute-start | bytes 491528 | tf_op jit(solution)/shard_map/cond/branch_0_fun/ppermute | solution.py:31
  37.3 7.9 %collective-permute-start.10 = (bf16[80,1024]{1,0:T(8,128)(2,1)S(1)}, bf16[80,1024]{1,0:T(8,128)(2,1)S(1)}, u32[]{:S(2)}, u32[]{:S(2)}) collective-permute-start(bf16[80,1024]{1,0:T(8,128)(2,1)S(1)} %fusion.35), channel_id=1, source_target_pairs={{1,0},{2,1},{3,2},{4,3},{5,4},{6,5},{7,6},{9,8},{10,9},{11,10},{12... | collective-permute-start | bytes 491528 | tf_op jit(solution)/shard_map/cond/branch_0_fun/ppermute | solution.py:31
  43.6 4.5 %collective-permute-start.11 = (bf16[80,1024]{1,0:T(8,128)(2,1)S(1)}, bf16[80,1024]{1,0:T(8,128)(2,1)S(1)}, u32[]{:S(2)}, u32[]{:S(2)}) collective-permute-start(bf16[80,1024]{1,0:T(8,128)(2,1)S(1)} %broadcast_select_fusion.3), channel_id=1, source_target_pairs={{1,0},{2,1},{3,2},{4,3},{5,4},{6,5},{7,6},{9,8},{10,9},{11,10},{12... | collective-permute-start | bytes 491528 | tf_op jit(solution)/shard_map/cond/branch_0_fun/ppermute | solution.py:31
  49.2 6.4 %collective-permute-start.12 = (bf16[96,1024]{1,0:T(8,128)(2,1)S(1)}, bf16[96,1024]{1,0:T(8,128)(2,1)S(1)}, u32[]{:S(2)}, u32[]{:S(2)}) collective-permute-start(bf16[96,1024]{1,0:T(8,128)(2,1)S(1)} %fusion.33), channel_id=1, source_target_pairs={{8,0},{9,1},{10,2},{11,3},{12,4},{13,5},{14,6},{15,7},{16,8},{17,9... | collective-permute-start | bytes 589832 | tf_op jit(solution)/shard_map/cond/branch_0_fun/ppermute | solution.py:31
  51.6 6.2 %collective-permute-start.13 = (bf16[96,1024]{1,0:T(8,128)(2,1)S(1)}, bf16[96,1024]{1,0:T(8,128)(2,1)S(1)}, u32[]{:S(2)}, u32[]{:S(2)}) collective-permute-start(bf16[96,1024]{1,0:T(8,128)(2,1)S(1)} %fusion.33), channel_id=1, source_target_pairs={{1,0},{2,1},{3,2},{4,3},{5,4},{6,5},{7,6},{9,8},{10,9},{11,10},{12... | collective-permute-start | bytes 589832 | tf_op jit(solution)/shard_map/cond/branch_0_fun/ppermute | solution.py:31
  55.7 5.3 %collective-permute-start.14 = (bf16[96,1024]{1,0:T(8,128)(2,1)S(1)}, bf16[96,1024]{1,0:T(8,128)(2,1)S(1)}, u32[]{:S(2)}, u32[]{:S(2)}) collective-permute-start(bf16[96,1024]{1,0:T(8,128)(2,1)S(1)} %broadcast_select_fusion.2), channel_id=1, source_target_pairs={{1,0},{2,1},{3,2},{4,3},{5,4},{6,5},{7,6},{9,8},{10,9},{11,10},{12... | collective-permute-start | bytes 589832 | tf_op jit(solution)/shard_map/cond/branch_0_fun/ppermute | solution.py:31
  62.2 7.7 %collective-permute-start.15 = (bf16[112,1024]{1,0:T(8,128)(2,1)S(1)}, bf16[112,1024]{1,0:T(8,128)(2,1)S(1)}, u32[]{:S(2)}, u32[]{:S(2)}) collective-permute-start(bf16[112,1024]{1,0:T(8,128)(2,1)S(1)} %fusion.31), channel_id=1, source_target_pairs={{8,0},{9,1},{10,2},{11,3},{12,4},{13,5},{14,6},{15,7},{16,8},{17,9... | collective-permute-start | bytes 688136 | tf_op jit(solution)/shard_map/cond/branch_0_fun/ppermute | solution.py:31
  66.2 6.1 %collective-permute-start.16 = (bf16[112,1024]{1,0:T(8,128)(2,1)S(1)}, bf16[112,1024]{1,0:T(8,128)(2,1)S(1)}, u32[]{:S(2)}, u32[]{:S(2)}) collective-permute-start(bf16[112,1024]{1,0:T(8,128)(2,1)S(1)} %fusion.31), channel_id=1, source_target_pairs={{1,0},{2,1},{3,2},{4,3},{5,4},{6,5},{7,6},{9,8},{10,9},{11,10},{12... | collective-permute-start | bytes 688136 | tf_op jit(solution)/shard_map/cond/branch_0_fun/ppermute | solution.py:31
  70.0 5.3 %collective-permute-start.17 = (bf16[112,1024]{1,0:T(8,128)(2,1)S(1)}, bf16[112,1024]{1,0:T(8,128)(2,1)S(1)}, u32[]{:S(2)}, u32[]{:S(2)}) collective-permute-start(bf16[112,1024]{1,0:T(8,128)(2,1)S(1)} %broadcast_select_fusion.1), channel_id=1, source_target_pairs={{1,0},{2,1},{3,2},{4,3},{5,4},{6,5},{7,6},{9,8},{10,9},{11,10},{12... | collective-permute-start | bytes 688136 | tf_op jit(solution)/shard_map/cond/branch_0_fun/ppermute | solution.py:31
  76.5 8.2 %collective-permute-start.18 = (bf16[128,1024]{1,0:T(8,128)(2,1)S(1)}, bf16[128,1024]{1,0:T(8,128)(2,1)S(1)}, u32[]{:S(2)}, u32[]{:S(2)}) collective-permute-start(bf16[128,1024]{1,0:T(8,128)(2,1)S(1)} %fusion.29), channel_id=1, source_target_pairs={{8,0},{9,1},{10,2},{11,3},{12,4},{13,5},{14,6},{15,7},{16,8},{17,9... | collective-permute-start | bytes 786440 | tf_op jit(solution)/shard_map/cond/branch_0_fun/ppermute | solution.py:31
  80.5 7.7 %collective-permute-start.19 = (bf16[128,1024]{1,0:T(8,128)(2,1)S(1)}, bf16[128,1024]{1,0:T(8,128)(2,1)S(1)}, u32[]{:S(2)}, u32[]{:S(2)}) collective-permute-start(bf16[128,1024]{1,0:T(8,128)(2,1)S(1)} %fusion.29), channel_id=1, source_target_pairs={{1,0},{2,1},{3,2},{4,3},{5,4},{6,5},{7,6},{9,8},{10,9},{11,10},{12... | collective-permute-start | bytes 786440 | tf_op jit(solution)/shard_map/cond/branch_0_fun/ppermute | solution.py:31
  84.8 7.3 %collective-permute-start.20 = (bf16[128,1024]{1,0:T(8,128)(2,1)S(1)}, bf16[128,1024]{1,0:T(8,128)(2,1)S(1)}, u32[]{:S(2)}, u32[]{:S(2)}) collective-permute-start(bf16[128,1024]{1,0:T(8,128)(2,1)S(1)} %broadcast_select_fusion), channel_id=1, source_target_pairs={{1,0},{2,1},{3,2},{4,3},{5,4},{6,5},{7,6},{9,8},{10,9},{11,10},{12... | collective-permute-start | bytes 786440 | tf_op jit(solution)/shard_map/cond/branch_0_fun/ppermute | solution.py:31
  93.3 1.0 %copy-start.1 = (bf16[1,1,128,1024]{3,2,1,0:T(8,128)(2,1)S(1)}, bf16[1,1,128,1024]{3,2,1,0:T(8,128)(2,1)}, u32[]{:S(2)}) copy-start(bf16[1,1,128,1024]{3,2,1,0:T(8,128)(2,1)} %param.7) | copy-start | bytes 786436
